TPU v7x, 32 devices: a whole 2x2x4 slice. The times are simulated.
32 devices in a mesh: chan: 8 (over z, y), facet: 4 (over x, core).
Axes of the slice: x: 2, y: 2, z: 4, core: 2. Of those that a mesh axis runs over, the one named last changes fastest.
Arguments:
- solution: float32 [8, 2048, 2048], P('chan', 'facet'), may hold values from -6 to 6
- residual: float32 [8, 2048, 2048], P('chan', 'facet'), may hold values from -120 to 120
- direction: float32 [8, 2048, 2048], P('chan', 'facet'), may hold values from -120 to 120
- spectra: float32 [8, 4096, 4096], P('chan', None, 'facet'), may hold values from 0.05 to 1
- basis: float32 [8, 8], replicated, may hold values from -2 to 2
- slot_channel: int32 [8], replicated, may hold values from 0 to 7, each once
Outputs:
- new_solution: float32 [8, 2048, 2048], P('chan', 'facet')
- new_residual: float32 [8, 2048, 2048], P('chan', 'facet')
- new_direction: float32 [8, 2048, 2048], P('chan', 'facet')
Inputs may be any that keep to these rules, and one draw needn't show every extreme that they name: `slot_channel`: every channel appears in exactly one slot.
All inputs are finite; a program needn't handle non-finite values.
Results may differ from a plain program's by a relative error of at most 0.000064.
Values sent between devices are 32-bit elements; how exact they have to be, the bound alone decides.
A program may use at most 256 MiB of HBM per device.

v0:
```python
import math

import jax
import jax.numpy as jnp
from jax import lax
from jax.sharding import PartitionSpec as P

ROOT = 64


HIGH = lax.Precision.HIGH
HIGHEST = lax.Precision.HIGHEST
PRIOR_FLOOR = 0.25


def wave(product, length, direction_sign):
    angles = (product % length).astype(jnp.float32) * (2.0 * math.pi / length)
    return (jnp.cos(angles), direction_sign * jnp.sin(angles))


def span(size):
    return jnp.arange(size, dtype=jnp.int32)


def swap_pairs(array, count, bit):
    pairs = [(place, place ^ bit) for place in range(count)]
    return lax.ppermute(array, "facet", pairs)


def column_table(width, columns, length, first_column):
    column = first_column + span(columns)[None, :]
    coarse = width // ROOT
    coarse_real, coarse_imag = wave(span(coarse)[:, None] * ROOT * column, length, -1.0)
    fine_real, fine_imag = wave(span(ROOT)[:, None] * column, length, -1.0)
    coarse_real, coarse_imag = (coarse_real[:, None], coarse_imag[:, None])
    fine_real, fine_imag = (fine_real[None], fine_imag[None])
    table_real = (coarse_real * fine_real - coarse_imag * fine_imag).reshape(width, columns)
    table_imag = (coarse_real * fine_imag + coarse_imag * fine_real).reshape(width, columns)
    return lax.optimization_barrier((table_real, table_imag))


def complex_stack(real, imag):
    return jnp.stack([jnp.stack([real, imag]), jnp.stack([-imag, real])])


def row_spectrum_pass(planes, spectrum, row_digits, factor):
    halved, columns = (row_digits.shape[0], planes.shape[2])
    blocks = planes.reshape(2, halved, factor, columns)
    first = complex_stack(*wave(row_digits[:, None] * span(factor)[None, :], factor, -1.0))
    section = jnp.einsum("pjnc,pqjk->kqnc", blocks, first, precision=HIGH)
    spread = span(factor)[:, None, None] * span(factor)[None, :, None] + (
        span(factor)[None, :, None] * span(factor)[None, None, :] * factor
    )
    second = complex_stack(*wave(spread, factor * factor, -1.0))
    freqs = jnp.einsum("kpnc,pqknj->kqjc", section, second, precision=HIGH)
    spectrum = spectrum.reshape(factor, factor, columns).transpose(1, 0, 2)
    weighted = freqs * spectrum[:, None]
    third = complex_stack(*wave(spread, factor * factor, 1.0))
    section = jnp.einsum("kpjc,pqknj->kqnc", weighted, third, precision=HIGH)
    last = complex_stack(*wave(row_digits[:, None] * span(factor)[None, :], factor, 1.0))
    rows = jnp.einsum("kpnc,pqjk->qjnc", section, last, precision=HIGH)
    return rows.reshape(2, halved * factor, columns)


def body(solution, residual, direction, spectra, basis, slot_channel):
    channel_count = basis.shape[0]
    factor = ROOT
    length = factor * factor
    facets = lax.axis_size("facet")
    place = lax.axis_index("facet")
    height, width = direction.shape[1:]
    columns = spectra.shape[2]
    own = direction[0]

    blocks = {0: own}
    bit = facets // 2
    while bit:
        blocks.update({key ^ bit: swap_pairs(blocks[key], facets, bit) for key in list(blocks)})
        bit //= 2
    table_real, table_imag = column_table(width, columns, length, place * columns)

    near = [blocks[key] for key in range(facets // 2)]
    far = [blocks[key] for key in range(facets // 2, facets)]
    near_rows = jnp.concatenate(near, axis=0)
    far_rows = jnp.concatenate(far, axis=0)
    planes = jnp.stack(
        [
            jnp.concatenate(
                [jnp.dot(part, table, precision=HIGH) for part in (near_rows, far_rows)], axis=0
            )
            for table in (table_real, table_imag)
        ]
    )
    digits = height // factor
    row_digits = ((place ^ span(facets))[:, None] * digits + span(digits)[None, :]).reshape(-1)
    rows = row_spectrum_pass(planes, spectra[0], row_digits, factor)

    def partial(part):
        wide = (((1,), (1,)), ((), ()))
        return lax.dot_general(part[0], table_real, wide, precision=HIGH) + lax.dot_general(
            part[1], table_imag, wide, precision=HIGH
        )

    sums = {}
    half = facets // 2
    for base in (half, 0):
        image = partial(rows[:, base * height : (base + half) * height])
        for key in range(half):
            sums[base + key] = image[key * height : (key + 1) * height]
    bit = 1
    while bit < facets:
        sums = {
            key: sums[key] + swap_pairs(sums[key | bit], facets, bit)
            for key in sorted(sums, reverse=True)
            if not key & bit
        }
        bit *= 2
    blurred = sums[0][None] * (1.0 / float(length * length))

    regrouped = lax.all_to_all(direction, "chan", split_axis=1, concat_axis=0, tiled=True)
    one_hot = (slot_channel[:, None] == span(channel_count)[None, :]).astype(jnp.float32)
    loadings = jnp.dot(one_hot, basis, precision=HIGHEST)
    coeffs = jnp.einsum("cq,cij->qij", loadings, regrouped, precision=HIGHEST)
    local_prior = PRIOR_FLOOR * regrouped + jnp.einsum(
        "cq,qij->cij", loadings, coeffs, precision=HIGHEST
    )
    prior_term = lax.all_to_all(local_prior, "chan", split_axis=0, concat_axis=1, tiled=True)
    applied = blurred + prior_term
    moments = jnp.stack(
        [
            jnp.sum(residual * residual),
            jnp.sum(direction * applied),
            jnp.sum(residual * applied),
            jnp.sum(applied * applied),
        ]
    )
    norm_now, curvature, cross, square = lax.psum(moments, ("chan", "facet"))
    step_size = norm_now / curvature
    new_solution = solution + step_size * direction
    new_residual = residual - step_size * applied
    norm_next = norm_now - 2.0 * step_size * cross + step_size * step_size * square
    new_direction = new_residual + norm_next / norm_now * direction
    return (new_solution, new_residual, new_direction)


def solution(mesh):
    return jax.shard_map(
        body,
        mesh=mesh,
        in_specs=(
            P("chan", "facet", None),
            P("chan", "facet", None),
            P("chan", "facet", None),
            P("chan", None, "facet"),
            P(),
            P(),
        ),
        out_specs=(P("chan", "facet", None), P("chan", "facet", None), P("chan", "facet", None)),
        check_vma=False,
    )
```

profile of v0, /device:TPU:0, one launch (start us, length us, event | category | flops | bytes accessed | tf_op | source)
XLA Modules:
  0.0 682.3 jit_solution(11598784250257221795)
XLA Ops:
  3.7 8.5 %copy.27 = f32[1,512,2048]{2,0,1:T(1,128)} copy(f32[1,512,2048]{2,1,0:T(8,128)} %param.8) | data formatting | bytes 8388608 | tf_op args[2]
  27.4 67.2 %collective-permute-done.1 = f32[512,2048]{1,0:T(8,128)} collective-permute-done((f32[512,2048]{1,0:T(8,128)}, f32[512,2048]{1,0:T(8,128)}, u32[]{:S(2)}, u32[]{:S(2)}) %collective-permute-start.1) | collective-permute-done | bytes 4194336 | tf_op jit(solution)/shard_map/ppermute | solution.py:27
  94.6 17.8 %copy.73 = f32[64,64,1024]{2,0,1:T(8,128)} copy(f32[64,64,1024]{2,1,0:T(8,128)} %bitcast.135) | data formatting | bytes 33554432 | tf_op jit(solution)/shard_map/reshape;squeeze | solution.py:56
  112.4 9.1 %fusion.41 = (f32[1,64,64,64]{2,3,1,0:T(8,128)S(1)}, f32[1,64,64,64]{2,3,1,0:T(8,128)S(1)}, f32[1,64,64,64]{2,3,1,0:T(8,128)S(1)}, f32[1,64,64,64]{2,3,1,0:T(8,128)S(1)}, f32[1,64,64,64]{2,3,1,0:T(8,128)}) fusion(s32[64,64]{0,1:T(8,128)S(1)} %broadcast_multiply_fusion.1, s32[64,64]{1,0:T(8,128)S(1)} %copy.17), kind=kLoop, calls=%fused_computation.73 | loop fusion | flops 4456448 | bytes 5275648 | tf_op jit(solution)/shard_map/sin | solution.py:18
  138.1 18.5 %fusion.17 = f32[1024,1024]{1,0:T(8,128)} fusion(f32[2048,1024]{1,0:T(8,128)} %bitcast.142, f32[512,2048]{1,0:T(8,128)} %collective-permute-done, f32[512,2048]{1,0:T(8,128)S(1)} %bitcast.129), kind=kOutput, calls=%fused_computation.26 | convolution fusion | flops 12886999040 | bytes 20971520 | tf_op jit(solution)/shard_map/dot_general | solution.py:89
  156.6 14.4 %fusion.16 = f32[1024,1024]{1,0:T(8,128)S(1)} fusion(f32[2048,1024]{1,0:T(8,128)S(1)} %bitcast.152, f32[512,2048]{1,0:T(8,128)} %collective-permute-done, f32[512,2048]{1,0:T(8,128)S(1)} %bitcast.130), kind=kOutput, calls=%fused_computation.25 | convolution fusion | flops 12886999040 | bytes 20971520 | tf_op jit(solution)/shard_map/dot_general | solution.py:89
  175.7 17.8 %fusion.79 = f32[1024,1024]{1,0:T(8,128)} fusion(f32[1024,2048]{1,0:T(8,128)} %constant_dynamic-update-slice_fusion, f32[2048,1024]{1,0:T(8,128)S(1)} %bitcast.147), kind=kOutput, calls=%fused_computation.140 | convolution fusion | flops 12884901888 | bytes 20971520 | tf_op jit(solution)/shard_map/dot_general | solution.py:89
  193.6 17.6 %fusion.80 = f32[1024,1024]{1,0:T(8,128)} fusion(f32[1024,2048]{1,0:T(8,128)} %constant_dynamic-update-slice_fusion, f32[2048,1024]{1,0:T(8,128)S(1)} %bitcast.153), kind=kOutput, calls=%fused_computation.141 | convolution fusion | flops 12884901888 | bytes 20971520 | tf_op jit(solution)/shard_map/dot_general | solution.py:89
  215.5 8.1 %copy.19 = f32[1,32,64,1024]{3,1,0,2:T(8,128)} copy(f32[1,32,64,1024]{3,2,1,0:T(8,128)S(1)} %bitcast.133) | data formatting | bytes 16777216 | tf_op jit(solution)/shard_map/stack | solution.py:86
  226.8 8.1 %copy.20 = f32[1,32,64,1024]{3,1,0,2:T(8,128)} copy(f32[1,32,64,1024]{3,2,1,0:T(8,128)S(1)} %bitcast.134) | data formatting | bytes 16777216 | tf_op jit(solution)/shard_map/stack | solution.py:86
  235.3 27.6 %convolution_bitcast_fusion = f32[64,2,64,1024,1]{3,0,2,1,4:T(8,128)} fusion(f32[1,32,64,1024]{3,1,0,2:T(8,128)} %copy.20, f32[1,32,64,1024]{3,1,0,2:T(8,128)} %copy.19, f32[1,2,32,64]{3,2,0,1:T(8,128)S(1)} %get-tuple-element.26, f32[1,2,32,64]{3,2,0,1:T(8,128)S(1)} %get-tuple-element.27), kind=kOutput, calls=%fused_computation.9 | convolution fusion | flops 3225427968 | bytes 50364416 | tf_op jit(solution)/shard_map/pjnc,pqjk->kqnc/dot_general | solution.py:50
  263.0 47.3 %fusion.4 = f32[64,2,64,1024,1]{3,2,1,0,4:T(8,128)} fusion(f32[64,2,64,1024,1]{3,0,2,1,4:T(8,128)} %convolution_bitcast_fusion, f32[2,2,64,64,64]{3,4,2,1,0:T(8,128)} %get-tuple-element.43), kind=kOutput, calls=%fused_computation.5 | convolution fusion | flops 6442450944 | bytes 71303168 | tf_op jit(solution)/shard_map/kpnc,pqknj->kqjc/dot_general | solution.py:55
  310.3 31.7 %fusion.11 = f32[64,2,64,1024]{3,2,1,0:T(8,128)} fusion(f32[64,2,64,1024,1]{3,2,1,0,4:T(8,128)} %fusion.4, f32[64,64,1024]{2,1,0:T(8,128)} %bitcast.126, f32[2,2,64,64,64]{3,4,2,1,0:T(8,128)} %get-tuple-element.42), kind=kOutput, calls=%fused_computation.15 | convolution fusion | flops 6450839552 | bytes 88080384 | tf_op jit(solution)/shard_map/kpjc,pqknj->kqnc/dot_general | solution.py:59
  342.0 40.1 %fusion.18 = f32[2,32,64,1024]{3,1,2,0:T(8,128)S(1)} fusion(f32[64,2,64,1024]{3,2,1,0:T(8,128)} %fusion.11, f32[1,2,32,64]{3,2,1,0:T(8,128)S(1)} %get-tuple-element.28, f32[1,2,32,64]{3,2,1,0:T(8,128)S(1)} %get-tuple-element.25), kind=kOutput, calls=%fused_computation.27 | convolution fusion | flops 3221233664 | bytes 50364416 | tf_op jit(solution)/shard_map/kpnc,pqjk->qjnc/dot_general | solution.py:61
  382.1 19.4 %copy.26 = f32[2,32,64,1024]{3,2,1,0:T(8,128)} copy(f32[2,32,64,1024]{3,1,2,0:T(8,128)S(1)} %fusion.18) | data formatting | bytes 33554432 | tf_op jit(solution)/shard_map/kpnc,pqjk->qjnc/dot_general | solution.py:61
  401.6 16.8 %fusion.25 = f32[1024,2048]{1,0:T(8,128)S(1)} fusion(f32[2048,1024]{1,0:T(8,128)} %bitcast.148, f32[2,2048,1024]{2,1,0:T(8,128)} %bitcast.136), kind=kOutput, calls=%fused_computation.38 | convolution fusion | flops 12884901888 | bytes 20971520 | tf_op jit(solution)/shard_map/dot_general | solution.py:100
  418.4 18.0 %fusion.37 = f32[1024,2048]{1,0:T(8,128)S(1)} fusion(f32[1024,2048]{1,0:T(8,128)S(1)} %fusion.25, f32[2048,1024]{1,0:T(8,128)} %bitcast.143, f32[2,2048,1024]{2,1,0:T(8,128)} %bitcast.137), kind=kOutput, calls=%fused_computation.65 | convolution fusion | flops 12886999040 | bytes 29360128 | tf_op jit(solution)/shard_map/dot_general | solution.py:100
  468.8 18.3 %fusion.30 = f32[1024,2048]{1,0:T(8,128)} fusion(f32[2048,1024]{1,0:T(8,128)} %bitcast.149, f32[2,2048,1024]{2,1,0:T(8,128)} %bitcast.138), kind=kOutput, calls=%fused_computation.46 | convolution fusion | flops 12884901888 | bytes 20971520 | tf_op jit(solution)/shard_map/dot_general | solution.py:100
  487.1 18.1 %fusion.36 = f32[1024,2048]{1,0:T(8,128)S(1)} fusion(f32[1024,2048]{1,0:T(8,128)} %fusion.30, f32[2048,1024]{1,0:T(8,128)} %bitcast.144, f32[2,2048,1024]{2,1,0:T(8,128)} %bitcast.139), kind=kOutput, calls=%fused_computation.64 | convolution fusion | flops 12886999040 | bytes 29360128 | tf_op jit(solution)/shard_map/dot_general | solution.py:100
  515.8 46.5 %all-to-all-done.1 = f32[8,64,2048]{2,1,0:T(8,128)} async-done(((f32[8,64,2048]{2,1,0:T(8,128)}), f32[8,64,2048]{2,1,0:T(8,128)}, u32[]{:S(2)}, u32[]{:S(2)}) %all-to-all-start.1) | async-done | bytes 4194336 | tf_op jit(solution)/shard_map/all_to_all | solution.py:127
  562.3 44.5 %collective-permute-done.5 = f32[512,2048]{1,0:T(8,128)} collective-permute-done((f32[512,2048]{1,0:T(8,128)}, f32[512,2048]{1,0:T(8,128)}, u32[]{:S(2)}, u32[]{:S(2)}) %collective-permute-start.5) | collective-permute-done | bytes 4194336 | tf_op jit(solution)/shard_map/ppermute | solution.py:27
  606.8 10.3 %multiply_reduce_fusion.1 = (f32[]{:T(128)}, f32[]{:T(128)}, f32[]{:T(128)}, f32[512,2048]{1,0:T(8,128)S(1)}) fusion(f32[1,512,2048]{2,1,0:T(8,128)} %param.7, f32[1,512,2048]{2,1,0:T(8,128)} %param.8, f32[8,64,2048]{2,1,0:T(8,128)} %all-to-all-done.1, f32[512,2048]{1,0:T(8,128)} %collective-permute-done.5, f32[512,2048]{1,0:T(8,128)} %collective-permute-done.3, ...), kind=kLoop, calls=%fused_computation.58 | loop fusion | flops 10485757 | bytes 29360140 | tf_op jit(solution)/shard_map/reduce_sum | solution.py:131
  623.5 41.0 %psum.7 = f32[4]{0:T(128)S(1)} all-reduce(f32[4]{0:T(128)S(1)} %pad_maximum_fusion.15), channel_id=1, replica_groups=mesh['chan'=8,'facet'=4] {'chan','facet'}, use_global_device_ids=true, to_apply=%region_4.5 | all-reduce | flops 4 | bytes 32 | tf_op jit(solution)/shard_map/psum | solution.py:137
  669.2 12.8 %multiply_add_fusion.1 = (f32[1,512,2048]{2,1,0:T(8,128)}, f32[1,512,2048]{2,1,0:T(8,128)}, f32[1,512,2048]{2,1,0:T(8,128)}) fusion(f32[1,512,2048]{2,1,0:T(8,128)} %param.8, f32[]{:T(128)S(6)} %div.7, f32[1,512,2048]{2,1,0:T(8,128)} %param.7, f32[512,2048]{1,0:T(8,128)} %copy-done.2, f32[]{:T(128)S(6)} %div.6, f32[1,512,2048]{2,1,0:T(8,128)} %param.6), kind=kLoop, calls=%fused_computation.54 | loop fusion | flops 6291456 | bytes 29360136 | tf_op jit(solution)/shard_map/add | solution.py:142
  (70 shorter events, 96.9 us)
Async XLA Ops:
  0.6 440.7 %copy-start = (f32[8,8]{1,0:T(8,128)S(1)}, f32[8,8]{1,0:T(8,128)}, u32[]{:S(2)}) copy-start(f32[8,8]{1,0:T(8,128)} %param.10) | copy-start | bytes 772
  0.6 93.9 %collective-permute-start.1 = (f32[512,2048]{1,0:T(8,128)}, f32[512,2048]{1,0:T(8,128)}, u32[]{:S(2)}, u32[]{:S(2)}) collective-permute-start(f32[512,2048]{1,0:T(8,128)} %bitcast.127), channel_id=1, source_target_pairs={{0,2},{1,3},{2,0},{3,1},{4,6},{5,7},{6,4},{7,5},{8,10},{9,11},{10,... | collective-permute-start | bytes 12582920 | tf_op jit(solution)/shard_map/ppermute | solution.py:27
  3.6 134.4 %collective-permute-start = (f32[512,2048]{1,0:T(8,128)}, f32[512,2048]{1,0:T(8,128)}, u32[]{:S(2)}, u32[]{:S(2)}) collective-permute-start(f32[512,2048]{1,0:T(8,128)} %bitcast.128), channel_id=1, source_target_pairs={{0,1},{1,0},{2,3},{3,2},{4,5},{5,4},{6,7},{7,6},{8,9},{9,8},{10,11... | collective-permute-start | bytes 12582920 | tf_op jit(solution)/shard_map/ppermute | solution.py:27
  12.2 429.3 %all-to-all-start = ((f32[1,512,2048]{2,0,1:T(1,128)}), f32[1,512,2048]{2,0,1:T(1,128)}, u32[]{:S(2)}, u32[]{:S(2)}) async-start(f32[1,512,2048]{2,0,1:T(1,128)} %copy.27), calls=%async_computation | async-start | bytes 8388608 | tf_op jit(solution)/shard_map/all_to_all | solution.py:120
  94.5 76.5 %collective-permute-start.2 = (f32[512,2048]{1,0:T(8,128)}, f32[512,2048]{1,0:T(8,128)}, u32[]{:S(2)}, u32[]{:S(2)}) collective-permute-start(f32[512,2048]{1,0:T(8,128)} %collective-permute-done.1), channel_id=1, source_target_pairs={{0,1},{1,0},{2,3},{3,2},{4,5},{5,4},{6,7},{7,6},{8,9},{9,8},{10,11... | collective-permute-start | bytes 12582920 | tf_op jit(solution)/shard_map/ppermute | solution.py:27
  133.1 5.0 copy-start.1
  133.1 23.5 %slice-start.4 = ((s8[8388608]{0:T(1024)(128)(4,1)}), s8[4194304]{0:T(1024)(128)(4,1)S(1)}, s32[]{:S(2)}) async-start(s8[8388608]{0:T(1024)(128)(4,1)} %bitcast.150), calls=%async_computation.6 | async-start | bytes 8388608
  138.0 18.5 %slice-start.5 = ((s8[8388608]{0:T(1024)(128)(4,1)}), s8[4194304]{0:T(1024)(128)(4,1)S(1)}, s32[]{:S(2)}) async-start(s8[8388608]{0:T(1024)(128)(4,1)} %bitcast.150), calls=%async_computation.7 | async-start | bytes 8388608
  138.1 37.7 %slice-start.2 = ((s8[8388608]{0:T(1024)(128)(4,1)}), s8[4194304]{0:T(1024)(128)(4,1)S(1)}, s32[]{:S(2)}) async-start(s8[8388608]{0:T(1024)(128)(4,1)} %bitcast.145), calls=%async_computation.4 | async-start | bytes 8388608
  156.6 19.1 %slice-start.3 = ((s8[8388608]{0:T(1024)(128)(4,1)}), s8[4194304]{0:T(1024)(128)(4,1)S(1)}, s32[]{:S(2)}) async-start(s8[8388608]{0:T(1024)(128)(4,1)} %bitcast.145), calls=%async_computation.5 | async-start | bytes 8388608
  436.3 4.5 copy-start.3
  436.3 5.0 copy-start.5
  440.8 67.6 %collective-permute-start.4 = (f32[512,2048]{1,0:T(8,128)}, f32[512,2048]{1,0:T(8,128)}, u32[]{:S(2)}, u32[]{:S(2)}) collective-permute-start(f32[512,2048]{1,0:T(8,128)} %slice.45), channel_id=1, source_target_pairs={{0,1},{1,0},{2,3},{3,2},{4,5},{5,4},{6,7},{7,6},{8,9},{9,8},{10,11... | collective-permute-start | bytes 12582920 | tf_op jit(solution)/shard_map/ppermute | solution.py:27
  462.7 99.6 %all-to-all-start.1 = ((f32[8,64,2048]{2,1,0:T(8,128)}), f32[8,64,2048]{2,1,0:T(8,128)}, u32[]{:S(2)}, u32[]{:S(2)}) async-start(f32[8,64,2048]{2,1,0:T(8,128)} %copy.31), calls=%async_computation.1 | async-start | bytes 8388608 | tf_op jit(solution)/shard_map/all_to_all | solution.py:127
  468.8 39.7 %slice-start = ((s8[8388608]{0:T(1024)(128)(4,1)}), s8[4194304]{0:T(1024)(128)(4,1)S(1)}, s32[]{:S(2)}) async-start(s8[8388608]{0:T(1024)(128)(4,1)} %bitcast.140), calls=%async_computation.2 | async-start | bytes 8388608
  487.1 21.3 %slice-start.1 = ((s8[8388608]{0:T(1024)(128)(4,1)}), s8[4194304]{0:T(1024)(128)(4,1)S(1)}, s32[]{:S(2)}) async-start(s8[8388608]{0:T(1024)(128)(4,1)} %bitcast.140), calls=%async_computation.3 | async-start | bytes 8388608
  505.2 3.2 copy-start.4
  508.5 7.3 %collective-permute-start.3 = (f32[512,2048]{1,0:T(8,128)S(1)}, f32[512,2048]{1,0:T(8,128)}, u32[]{:S(2)}, u32[]{:S(2)}) collective-permute-start(f32[512,2048]{1,0:T(8,128)S(1)} %slice.41), channel_id=1, source_target_pairs={{0,1},{1,0},{2,3},{3,2},{4,5},{5,4},{6,7},{7,6},{8,9},{9,8},{10,11... | collective-permute-start | bytes 12582920 | tf_op jit(solution)/shard_map/ppermute | solution.py:27
  513.5 93.3 %collective-permute-start.5 = (f32[512,2048]{1,0:T(8,128)}, f32[512,2048]{1,0:T(8,128)}, u32[]{:S(2)}, u32[]{:S(2)}) collective-permute-start(f32[512,2048]{1,0:T(8,128)} %slice_add_fusion), channel_id=1, source_target_pairs={{0,2},{1,3},{2,0},{3,1},{4,6},{5,7},{6,4},{7,5},{8,10},{9,11},{10,... | collective-permute-start | bytes 12582920 | tf_op jit(solution)/shard_map/ppermute | solution.py:27
  617.2 2.0 copy-start.2
where the time goes:
time: 687 us; the launch traced here: 682 us
  matrix products  299 us (44%)
  waiting for transfers between devices  159 us (23%)
  local copies, waits for them, and re-layouts  90.7 us (13%)
  other arithmetic  69.8 us (10%)
  blocking collectives  41 us (6%)
  starting transfers between devices  17.1 us (2%)
    ppermute x6, waiting for transfers between devices, swap_pairs(): return lax.ppermute(array, 'facet', pairs)  112 us
    dot_general x4, matrix products, body(): jnp.dot(part, table, precision=HIGH)  68.4 us
    dot_general x1, matrix products, row_spectrum_pass(): freqs = jnp.einsum('kpnc,pqknj->kqjc', section, second, precision=HIGH)  47.3 us
    all_to_all x1, waiting for transfers between devices, body(): lax.all_to_all(local_prior, 'chan', split_axis=0, concat_axis=1, tiled=True)  46.5 us
    psum x1, blocking collectives, body(): norm_now, curvature, cross, square = lax.psum(moments, ('chan', 'facet'))  41 us
    dot_general x1, matrix products, row_spectrum_pass(): rows = jnp.einsum('kpnc,pqjk->qjnc', section, last, precision=HIGH)  40.1 us
    dot_general x2, matrix products, partial(): lax.dot_general(part[0], table_real, wide, precision=HIGH)  36 us
    dot_general x2, matrix products, partial(): lax.dot_general(part[1], table_imag, wide, precision=HIGH)  35.1 us
  transfers between devices with their start and end apart: 8, of which 4 were waited for; matrix products, arithmetic and copies ran while one was open for 62% of the time, Pallas kernels for 0%

commit v1 on v0

v1 whole, which is shorter than its diff:
```python
import functools
import math

import jax
import jax.numpy as jnp
import ml_dtypes
import numpy as np
from jax import lax
from jax.experimental import pallas as pl
from jax.experimental.pallas import tpu as pltpu
from jax.sharding import PartitionSpec as P

RADIX = 32
FINE = 128
ROOT = 64
LANES = 128
TILE = 256
HIGHEST = lax.Precision.HIGHEST
PRIOR_FLOOR = 0.25
HALF = math.sqrt(0.5)
MESH = pl.DeviceIdType.MESH


def np_split(table):
    high = table.astype(ml_dtypes.bfloat16)
    low = (table - high.astype(np.float64)).astype(ml_dtypes.bfloat16)
    return high, low


@functools.cache
def row_tables():
    length = RADIX * FINE
    coarse = np.arange(RADIX)[:, None, None]
    fine = np.arange(FINE)[None, :, None]
    place = np.arange(FINE)[None, None, :]
    angle = -2.0 * np.pi * ((place * (RADIX * fine + coarse)) % length) / length
    real, imag = np.cos(angle), np.sin(angle)
    forward = np.concatenate(
        [np.concatenate([real, -imag], axis=2), np.concatenate([imag, real], axis=2)], axis=1
    )
    inverse = np.transpose(forward, (0, 2, 1)) / float(length * length)
    return np_split(forward) + np_split(inverse)


@functools.cache
def column_factors(width, length):
    column = np.arange(length)[None, :]

    def wave(rows):
        angle = -2.0 * np.pi * ((rows[:, None] * column) % length) / length
        return np.cos(angle).astype(np.float32), np.sin(angle).astype(np.float32)

    return wave(np.arange(width // ROOT) * ROOT) + wave(np.arange(ROOT))


def split(values):
    high = values.astype(jnp.bfloat16)
    low = (values - high.astype(jnp.float32)).astype(jnp.bfloat16)
    return high, low


def turn(real, imag, num, den, sign):
    num %= den
    if (num * 8) % den == 0:
        eighth = (sign * (num * 8 // den)) % 8
        if eighth == 0:
            return real, imag
        if eighth == 1:
            return (real - imag) * HALF, (real + imag) * HALF
        if eighth == 2:
            return -imag, real
        if eighth == 3:
            return (real + imag) * -HALF, (real - imag) * HALF
        if eighth == 4:
            return -real, -imag
        if eighth == 5:
            return (imag - real) * HALF, (real + imag) * -HALF
        if eighth == 6:
            return imag, -real
        return (real + imag) * HALF, (imag - real) * HALF
    c = math.cos(2.0 * math.pi * num / den)
    s = sign * math.sin(2.0 * math.pi * num / den)
    return real * c - imag * s, real * s + imag * c


def fft(points, sign):
    count = len(points)
    if count == 1:
        return points
    half = count // 2
    even, odd = [], []
    for i in range(half):
        (ar, ai), (br, bi) = points[i], points[i + half]
        even.append((ar + br, ai + bi))
        if 4 * i == count:
            odd.append((ai - bi, br - ar) if sign < 0 else (bi - ai, ar - br))
        else:
            odd.append(turn(ar - br, ai - bi, i, count, sign))
    result = [None] * count
    result[0::2] = fft(even, sign)
    result[1::2] = fft(odd, sign)
    return result


def dot3(table_high, table_low, values):
    high, low = split(values)
    dot = functools.partial(jnp.dot, preferred_element_type=jnp.float32)
    return dot(table_high, high) + dot(table_low, high) + dot(table_high, low)


def row_kernel(slot_ref, planes_ref, *refs):
    lanes = planes_ref.shape[2] // LANES
    spectra = refs[:lanes]
    forward_high, forward_low, inverse_high, inverse_low, _, out_ref, work = refs[lanes:]
    used = RADIX // 2
    slots = [slot_ref[a] * FINE for a in range(used)]
    steps = FINE // 8 * lanes

    def position(step):
        col = pl.ds(pl.multiple_of(step % lanes * LANES, LANES), LANES)
        return step // lanes * 8, col

    def rows(base, at):
        return pl.ds(pl.multiple_of(base + at, 8), 8)

    def forward(step, _):
        at, col = position(step)
        points = [(planes_ref[0, rows(s, at), col], planes_ref[1, rows(s, at), col]) for s in slots]
        for k, (real, imag) in enumerate(fft(points, -1)):
            work[2 * k, rows(0, at), col] = real
            work[2 * k, rows(FINE, at), col] = imag
        points = [turn(*point, a, RADIX, -1) for a, point in enumerate(points)]
        for k, (real, imag) in enumerate(fft(points, -1)):
            work[2 * k + 1, rows(0, at), col] = real
            work[2 * k + 1, rows(FINE, at), col] = imag
        return 0

    lax.fori_loop(0, steps, forward, 0)

    def middle(k, _):
        freqs = dot3(forward_high[k], forward_low[k], work[k])
        weight = jnp.concatenate(
            [ref[pl.ds(k, FINE, stride=RADIX), :] for ref in spectra], axis=1
        )
        freqs = freqs * jnp.concatenate([weight, weight], axis=0)
        work[k] = dot3(inverse_high[k], inverse_low[k], freqs)
        return 0

    lax.fori_loop(0, RADIX, middle, 0, unroll=16)

    def inverse(step, _):
        at, col = position(step)

        def side(odd):
            points = [
                (work[2 * k + odd, rows(0, at), col], work[2 * k + odd, rows(FINE, at), col])
                for k in range(used)
            ]
            return fft(points, 1)

        even, odd = side(0), side(1)
        for a, s in enumerate(slots):
            real, imag = turn(*odd[a], a, RADIX, 1)
            out_ref[0, rows(s, at), col] = even[a][0] + real
            out_ref[1, rows(s, at), col] = even[a][1] + imag
        return 0

    lax.fori_loop(0, steps, inverse, 0)


def row_pass(planes, spectrum, slots, after):
    _, height, columns = planes.shape
    tables = [jnp.asarray(table) for table in row_tables()]
    lanes = TILE // LANES
    whole = pl.BlockSpec(
        (RADIX, 2 * FINE, 2 * FINE), lambda i, s: (0, 0, 0), pipeline_mode=pl.Buffered(1)
    )
    tile = pl.BlockSpec((2, height, TILE), lambda i, s: (0, 0, i))
    strips = [
        pl.BlockSpec((2 * height, LANES), lambda i, s, c=c: (0, i * lanes + c))
        for c in range(lanes)
    ]
    return pl.pallas_call(
        row_kernel,
        grid_spec=pltpu.PrefetchScalarGridSpec(
            num_scalar_prefetch=1,
            grid=(columns // TILE,),
            in_specs=[tile] + strips + [whole] * 4 + [pl.BlockSpec(memory_space=pl.ANY)],
            out_specs=tile,
            scratch_shapes=[pltpu.VMEM((RADIX, 2 * FINE, TILE), jnp.float32)],
        ),
        out_shape=jax.ShapeDtypeStruct(planes.shape, jnp.float32),
        compiler_params=pltpu.CompilerParams(vmem_limit_bytes=60 << 20),
        cost_estimate=pl.CostEstimate(
            flops=6 * 2 * 256 * RADIX * 256 * columns, bytes_accessed=64 << 20, transcendentals=0
        ),
        name="row_pass",
    )(slots, planes, *([spectrum] * lanes), *tables, after)


def table_kernel(place_ref, coarse_real, coarse_imag, fine_real, fine_imag, high_ref, low_ref):
    columns = fine_real.shape[1]
    row = pl.ds(pl.program_id(0) % 8, 1)
    cr, ci = coarse_real[row, :], coarse_imag[row, :]
    fr, fi = fine_real[...], fine_imag[...]
    high_ref[:, :columns], low_ref[:, :columns] = split(cr * fr - ci * fi)
    high_ref[:, columns:], low_ref[:, columns:] = split(cr * fi + ci * fr)


def width_table(width, columns, length, place):
    factors = [jnp.asarray(factor) for factor in column_factors(width, length)]
    coarse = pl.BlockSpec((8, columns), lambda i, p: (i // 8, p[0]))
    fine = pl.BlockSpec((ROOT, columns), lambda i, p: (0, p[0]))
    out = pl.BlockSpec((ROOT, 2 * columns), lambda i, p: (i, 0))
    return pl.pallas_call(
        table_kernel,
        grid_spec=pltpu.PrefetchScalarGridSpec(
            num_scalar_prefetch=1,
            grid=(width // ROOT,),
            in_specs=[coarse, coarse, fine, fine],
            out_specs=[out, out],
        ),
        out_shape=[jax.ShapeDtypeStruct((width, 2 * columns), jnp.bfloat16)] * 2,
        cost_estimate=pl.CostEstimate(
            flops=20 * width * columns, bytes_accessed=8 * width * columns, transcendentals=0
        ),
        name="width_table",
    )(place.reshape(1), *factors)


def width_kernel(count, *refs):
    blocks = refs[:count]
    table_high, table_low = refs[count : count + 2]
    out_ref, high_ref, low_ref = refs[-3:]

    @pl.when(pl.program_id(0) == 0)
    def _():
        base = 0
        for ref in blocks:
            rows = ref.shape[0]
            high_ref[base : base + rows], low_ref[base : base + rows] = split(ref[...])
            base += rows

    dot = functools.partial(jnp.dot, preferred_element_type=jnp.float32)
    high, low = high_ref[...], low_ref[...]
    weight = table_high[...]
    out_ref[0] = dot(high, weight) + dot(low, weight) + dot(high, table_low[...])


def width_forward(blocks, tables, planes, first, columns, height):
    width = blocks[0].shape[1]
    total = sum(block.shape[0] for block in blocks)
    tiles = columns // TILE
    before = [] if planes is None else [planes]
    table = pl.BlockSpec((width, TILE), lambda n: (0, n))
    return pl.pallas_call(
        functools.partial(width_kernel, len(blocks)),
        grid=(2 * tiles,),
        in_specs=[pl.BlockSpec(block.shape, lambda n: (0, 0)) for block in blocks]
        + [table, table]
        + [pl.BlockSpec(memory_space=pl.ANY)] * len(before),
        out_specs=pl.BlockSpec(
            (1, total, TILE), lambda n: (n // tiles, first // total, n % tiles)
        ),
        out_shape=jax.ShapeDtypeStruct((2, height, columns), jnp.float32),
        scratch_shapes=[pltpu.VMEM((total, width), jnp.bfloat16)] * 2,
        input_output_aliases={len(blocks) + 2: 0} if before else {},
        compiler_params=pltpu.CompilerParams(vmem_limit_bytes=48 << 20),
        cost_estimate=pl.CostEstimate(
            flops=12 * total * width * columns,
            bytes_accessed=8 * width * columns + 4 * total * (width + 2 * columns),
            transcendentals=0,
        ),
        name="width_forward",
    )(*blocks, *tables, *before)


def back_kernel(count, planes_ref, table_high, table_low, _, *refs):
    outs = refs[:count]
    high_ref, low_ref = refs[count:]
    columns = planes_ref.shape[2]

    @pl.when(pl.program_id(0) == 0)
    def _():
        for part in range(2):
            col = slice(part * columns, (part + 1) * columns)
            high_ref[:, col], low_ref[:, col] = split(planes_ref[part])

    wide = (((1,), (1,)), ((), ()))
    dot = functools.partial(
        lax.dot_general, dimension_numbers=wide, preferred_element_type=jnp.float32
    )
    high, low = high_ref[...], low_ref[...]
    weight = table_high[...]
    image = dot(high, weight) + dot(low, weight) + dot(high, table_low[...])
    base = 0
    for ref in outs:
        rows = ref.shape[0]
        ref[...] = image[base : base + rows]
        base += rows


def width_back(planes, tables, first, sizes, after):
    _, _, columns = planes.shape
    width = tables[0].shape[0]
    total = sum(sizes)
    table = pl.BlockSpec((TILE, 2 * columns), lambda n: (n, 0))
    return pl.pallas_call(
        functools.partial(back_kernel, len(sizes)),
        grid=(width // TILE,),
        in_specs=[
            pl.BlockSpec((2, total, columns), lambda n: (0, first // total, 0)),
            table,
            table,
            pl.BlockSpec(memory_space=pl.ANY),
        ],
        out_specs=[pl.BlockSpec((rows, TILE), lambda n: (0, n)) for rows in sizes],
        out_shape=[jax.ShapeDtypeStruct((rows, width), jnp.float32) for rows in sizes],
        scratch_shapes=[pltpu.VMEM((total, 2 * columns), jnp.bfloat16)] * 2,
        compiler_params=pltpu.CompilerParams(vmem_limit_bytes=48 << 20),
        cost_estimate=pl.CostEstimate(
            flops=12 * total * width * columns,
            bytes_accessed=8 * width * columns + 4 * total * (width + 2 * columns),
            transcendentals=0,
        ),
        name="width_back",
    )(planes, *tables, after)


def prior_kernel(gram_ref, cube_ref, out_ref):
    count = cube_ref.shape[0]
    for c in range(count):
        total = gram_ref[c, 0] * cube_ref[0]
        for k in range(1, count):
            total = total + gram_ref[c, k] * cube_ref[k]
        out_ref[c] = total


def prior_term(cube, gram):
    count, rows, width = cube.shape
    block = pl.BlockSpec((count, 8, width), lambda i: (0, i, 0))
    return pl.pallas_call(
        prior_kernel,
        grid=(rows // 8,),
        in_specs=[pl.BlockSpec(memory_space=pltpu.SMEM), block],
        out_specs=block,
        out_shape=jax.ShapeDtypeStruct(cube.shape, jnp.float32),
        cost_estimate=pl.CostEstimate(
            flops=2 * count * cube.size, bytes_accessed=8 * cube.size, transcendentals=0
        ),
        name="prior_term",
    )(gram, cube)


def moment_kernel(terms, *refs):
    parts = refs[:terms]
    residual_ref, direction_ref = refs[terms : terms + 2]
    applied_ref, moment_ref = refs[-2:]

    @pl.when(pl.program_id(0) == 0)
    def _():
        moment_ref[...] = jnp.zeros_like(moment_ref)

    applied = parts[0][...]
    for ref in parts[1:]:
        applied = applied + ref[...]
    applied_ref[...] = applied
    residual, direction = residual_ref[...], direction_ref[...]
    width = applied.shape[1]

    def fold(product):
        total = product[:8]
        for at in range(8, product.shape[0], 8):
            total = total + product[at : at + 8]
        folded = total[:, :LANES]
        for at in range(LANES, width, LANES):
            folded = folded + total[:, at : at + LANES]
        return folded

    moment_ref[0] += fold(residual * residual)
    moment_ref[1] += fold(direction * applied)
    moment_ref[2] += fold(residual * applied)
    moment_ref[3] += fold(applied * applied)


def moments_of(wide, chunk, residual, direction, applied, first):
    rows, width = chunk[0].shape
    step = 64 if rows % 64 == 0 else rows
    at = first // step
    here = pl.BlockSpec((step, width), lambda i: (at + i, 0))
    own = pl.BlockSpec((step, width), lambda i: (i, 0))
    terms = len(wide) + len(chunk)
    before = [] if applied is None else [applied]
    return pl.pallas_call(
        functools.partial(moment_kernel, terms),
        grid=(rows // step,),
        in_specs=[here] * len(wide)
        + [own] * len(chunk)
        + [here, here]
        + [pl.BlockSpec(memory_space=pl.ANY)] * len(before),
        out_specs=[here, pl.BlockSpec((4, 8, LANES), lambda i: (0, 0, 0))],
        out_shape=[
            jax.ShapeDtypeStruct(residual.shape, jnp.float32),
            jax.ShapeDtypeStruct((4, 8, LANES), jnp.float32),
        ],
        input_output_aliases={terms + 2: 0} if before else {},
        cost_estimate=pl.CostEstimate(
            flops=10 * rows * width,
            bytes_accessed=4 * (terms + 3) * rows * width,
            transcendentals=0,
        ),
        name="moments",
    )(*wide, *chunk, residual, direction, *before)


def reduce_kernel(axes, sizes, parts, *refs):
    inputs = refs[:parts]
    out_ref, mine, landed, send_sem, recv_sem = refs[parts:]
    barrier = pltpu.get_barrier_semaphore()

    def peers(axis):
        size = sizes[axis]
        me = lax.axis_index(axes[axis])
        return [lax.rem(me + hop, size) for hop in range(1, size)]

    for axis in range(2):
        for peer in peers(axis):
            pl.semaphore_signal(barrier, inc=1, device_id={axes[axis]: peer}, device_id_type=MESH)
    total = inputs[0][...]
    for ref in inputs[1:]:
        total = total + ref[...]
    pl.semaphore_wait(barrier, sizes[0] + sizes[1] - 2)
    slot = 0
    for axis in range(2):
        mine[axis] = total
        copies = []
        for hop, peer in enumerate(peers(axis)):
            copies.append(
                pltpu.make_async_remote_copy(
                    src_ref=mine.at[axis],
                    dst_ref=landed.at[slot + hop],
                    send_sem=send_sem.at[slot + hop],
                    recv_sem=recv_sem.at[slot + hop],
                    device_id={axes[axis]: peer},
                    device_id_type=MESH,
                )
            )
        for copy in copies:
            copy.start()
        for hop, copy in enumerate(copies):
            copy.wait()
        me = lax.axis_index(axes[axis])
        size = sizes[axis]
        total = jnp.zeros_like(total)
        for source in range(size):
            hop = lax.rem(me - source + size, size)
            got = landed[slot + jnp.maximum(hop, 1) - 1]
            total = total + jnp.where(hop == 0, mine[axis], got)
        slot += size - 1
    sums = jnp.sum(jnp.sum(total, axis=2, keepdims=True), axis=1, keepdims=True)
    out_ref[...] = jnp.broadcast_to(sums, total.shape)


def reduce_moments(moments, axes, sizes):
    shape = moments[0].shape
    slots = sizes[0] + sizes[1] - 2
    return pl.pallas_call(
        functools.partial(reduce_kernel, axes, sizes, len(moments)),
        out_shape=jax.ShapeDtypeStruct(shape, jnp.float32),
        in_specs=[pl.BlockSpec(memory_space=pltpu.VMEM)] * len(moments),
        out_specs=pl.BlockSpec(memory_space=pltpu.VMEM),
        scratch_shapes=[
            pltpu.VMEM((2,) + shape, jnp.float32),
            pltpu.VMEM((slots,) + shape, jnp.float32),
            pltpu.SemaphoreType.DMA((slots,)),
            pltpu.SemaphoreType.DMA((slots,)),
        ],
        compiler_params=pltpu.CompilerParams(collective_id=0, has_side_effects=True),
        name="reduce_moments",
    )(*moments)


def update_kernel(
    sum_ref, solution_ref, residual_ref, direction_ref, applied_ref, x_ref, r_ref, d_ref
):
    def scalar(at):
        return sum_ref[at, 0:1, 0:1]

    norm_now, curvature, cross, square = [scalar(at) for at in range(4)]
    step_size = norm_now / curvature
    norm_next = norm_now - 2.0 * step_size * cross + step_size * step_size * square
    ratio = norm_next / norm_now
    direction = direction_ref[...]
    x_ref[...] = solution_ref[...] + step_size * direction
    residual = residual_ref[...] - step_size * applied_ref[...]
    r_ref[...] = residual
    d_ref[...] = residual + ratio * direction


def update(sums, solution, residual, direction, applied):
    height, width = applied.shape
    step = 64
    block = pl.BlockSpec((step, width), lambda i: (i, 0))
    return pl.pallas_call(
        update_kernel,
        grid=(height // step,),
        in_specs=[pl.BlockSpec(sums.shape, lambda i: (0, 0, 0))] + [block] * 4,
        out_specs=[block] * 3,
        out_shape=[jax.ShapeDtypeStruct((height, width), jnp.float32)] * 3,
        cost_estimate=pl.CostEstimate(
            flops=6 * height * width, bytes_accessed=28 * height * width, transcendentals=0
        ),
        name="update",
    )(sums, solution, residual, direction, applied)


def swap_pairs(array, count, bit):
    pairs = [(place, place ^ bit) for place in range(count)]
    return lax.ppermute(array, "facet", pairs)


def body(solution, residual, direction, spectra, basis, slot_channel):
    channel_count = basis.shape[0]
    length = RADIX * FINE
    facets = lax.axis_size("facet")
    place = lax.axis_index("facet")
    height, width = direction.shape[1:]
    columns = spectra.shape[2]
    own = direction[0]
    top = facets // 2
    per_facet = height // FINE

    stacked = own.reshape(channel_count, height // channel_count, width)
    regrouped = lax.all_to_all(stacked, "chan", split_axis=0, concat_axis=0, tiled=True)
    one_hot = (
        slot_channel[:, None] == jnp.arange(channel_count, dtype=jnp.int32)[None, :]
    ).astype(jnp.float32)
    loadings = jnp.dot(one_hot, basis, precision=HIGHEST)
    gram = jnp.einsum("cq,dq->cd", loadings, loadings, precision=HIGHEST)
    gram = gram + PRIOR_FLOOR * jnp.eye(channel_count, dtype=jnp.float32)

    chunks = [own[at * FINE : (at + 1) * FINE] for at in range(per_facet)]
    far = []
    for chunk in chunks:
        blocks = {top: swap_pairs(chunk, facets, top)}
        bit = top // 2
        while bit:
            blocks.update({key ^ bit: swap_pairs(blocks[key], facets, bit) for key in list(blocks)})
            bit //= 2
        far.append(blocks)
    near = {0: own}
    bit = top // 2
    while bit:
        near.update({key ^ bit: swap_pairs(near[key], facets, bit) for key in list(near)})
        bit //= 2

    groups = []
    if per_facet > 1:
        groups += [([near[key]], [(key, s) for s in range(per_facet)]) for key in range(top)]
    else:
        groups.append(([near[key] for key in range(top)], [(key, 0) for key in range(top)]))
    for s, blocks in enumerate(far):
        keys = range(top, facets)
        groups.append(([blocks[key] for key in keys], [(key, s) for key in keys]))
    order = [entry for _, entries in groups for entry in entries]
    slot_of = np.zeros((facets, per_facet), np.int32)
    for at, (key, s) in enumerate(order):
        slot_of[key, s] = at
    slots = jnp.asarray(slot_of)[jnp.arange(facets, dtype=jnp.int32) ^ place].reshape(-1)

    tables = width_table(width, columns, length, place)
    planes = None
    first = 0
    starts = []
    for blocks, entries in groups:
        planes = width_forward(blocks, tables, planes, first, columns, facets * height)
        starts.append(first)
        first += len(entries) * FINE

    local_prior = prior_term(regrouped, gram)
    prior = lax.all_to_all(local_prior, "chan", split_axis=0, concat_axis=0, tiled=True)
    prior = prior.reshape(height, width)

    rows = row_pass(planes, spectra[0], slots, local_prior)

    after = rows
    arrived = []
    near_sums = {}
    for (blocks, entries), start in list(zip(groups, starts))[::-1]:
        if entries[0][0] < top:
            continue
        sizes = [FINE] * len(entries)
        parts = width_back(rows, tables, start, sizes, after)
        after = parts[0]
        sums = {key: part for (key, _), part in zip(entries, parts)}
        bit = 1
        while bit < top:
            sums = {
                key: sums[key] + swap_pairs(sums[key | bit], facets, bit)
                for key in sorted(sums, reverse=True)
                if not key & bit
            }
            bit *= 2
        arrived.append((entries[0][1], swap_pairs(sums[top], facets, top)))
    for (blocks, entries), start in list(zip(groups, starts))[::-1]:
        if entries[0][0] >= top:
            continue
        if per_facet > 1:
            key = entries[0][0]
            near_sums[key] = width_back(rows, tables, start, [height], after)[0]
            after = near_sums[key]
        else:
            parts = width_back(rows, tables, start, [FINE] * len(entries), after)
            near_sums = {key: part for (key, _), part in zip(entries, parts)}
    bit = 1
    while 2 * bit < top:
        near_sums = {
            key: near_sums[key] + swap_pairs(near_sums[key | bit], facets, bit)
            for key in sorted(near_sums, reverse=True)
            if not key & bit
        }
        bit *= 2
    wide = [near_sums[0], swap_pairs(near_sums[bit], facets, bit), prior]

    applied = None
    moments = []
    for s, part in arrived:
        applied, moment = moments_of(wide, [part], residual[0], own, applied, s * FINE)
        moments.append(moment)
    sizes = (lax.axis_size("chan"), facets)
    sums = reduce_moments(moments, ("chan", "facet"), sizes)
    results = update(sums, solution[0], residual[0], own, applied)
    return tuple(result[None] for result in results)


def solution(mesh):
    return jax.shard_map(
        body,
        mesh=mesh,
        in_specs=(
            P("chan", "facet", None),
            P("chan", "facet", None),
            P("chan", "facet", None),
            P("chan", None, "facet"),
            P(),
            P(),
        ),
        out_specs=(P("chan", "facet", None), P("chan", "facet", None), P("chan", "facet", None)),
        check_vma=False,
    )
```

time: 687 us -> 485 us (0.71)
  Pallas kernels: 0 us -> 321 us
  matrix products: 299 us -> 0.92 us
  local copies, waits for them, and re-layouts: 90.7 us -> 12.6 us
  other arithmetic: 69.8 us -> 2.47 us
  blocking collectives: 41 us -> 0 us
  waiting for transfers between devices: 159 us -> 122 us
    pallas_call x0 -> x21, Pallas kernels: none -> 321 us  [the longest x6 88.9 us: width_forward(): pl.pallas_call(functools.partial(width_kernel, len(blocks)), grid=(2 * ti...]
    dot_general x14 -> x1, matrix products: 299 us -> 0.74 us  [body(): gram = jnp.einsum('cq,dq->cd', loadings, loadings, precision=HIGHEST)]
    all_to_all x2, waiting for transfers between devices: 46.5 us -> 0.01 us  [the longest x1 0.01 us: body(): lax.all_to_all(local_prior, 'chan', split_axis=0, concat_axis=0, tiled=True)]
    psum x1 -> x0, blocking collectives: 41 us -> none  [body(): norm_now, curvature, cross, square = lax.psum(moments, ('chan', 'facet'))]
    another operation x4 -> x0, local copies, waits for them, and re-layouts: 34.5 us -> none  [the longest x1 17.8 us: row_spectrum_pass(): spectrum = spectrum.reshape(factor, factor, columns).transpose(1, 0, 2)]
    add x4 -> x0, other arithmetic: 20 us -> none  [the longest x1 12.8 us: body(): new_direction = new_residual + norm_next / norm_now * direction]
    dot_general x1 -> x0, local copies, waits for them, and re-layouts: 19.4 us -> none  [row_spectrum_pass(): rows = jnp.einsum('kpnc,pqjk->qjnc', section, last, precision=HIGH)]
    unnamed x27 -> x20, local copies, waits for them, and re-layouts: 24.7 us -> 7.13 us
  transfers between devices with their start and end apart: 8 -> 20, of which waited for: 4 -> 6; matrix products, arithmetic and copies ran while one was open for 62% -> 2% of each run, Pallas kernels for 0% -> 59%
where the time goes in v1:
time: 485 us; the launch traced here: 483 us
  Pallas kernels  321 us (66%)
  waiting for transfers between devices  122 us (25%)
  starting transfers between devices  23.6 us (5%)
  local copies, waits for them, and re-layouts  12.6 us (3%)
    ppermute x18, waiting for transfers between devices, swap_pairs(): return lax.ppermute(array, 'facet', pairs)  122 us
    pallas_call x6, Pallas kernels, width_forward(): pl.pallas_call(functools.partial(width_kernel, len(blocks)), grid=(2 * ti...  88.9 us
    pallas_call x6, Pallas kernels, width_back(): pl.pallas_call(functools.partial(back_kernel, len(sizes)), grid=(width //...  87.7 us
    pallas_call x1, Pallas kernels, row_pass(): pl.pallas_call(row_kernel, grid_spec=pltpu.PrefetchScalarGridSpec(num_sca...  79.7 us
    pallas_call x1, Pallas kernels, width_table(): pl.pallas_call(table_kernel, grid_spec=pltpu.PrefetchScalarGridSpec(num_s...  16 us
    pallas_call x4, Pallas kernels, moments_of(): pl.pallas_call(functools.partial(moment_kernel, terms), grid=(rows // ste...  15.2 us
    pallas_call x1, Pallas kernels, reduce_moments(): pl.pallas_call(functools.partial(reduce_kernel, axes, sizes, len(moments)...  13.8 us
    pallas_call x1, Pallas kernels, update(): pl.pallas_call(update_kernel, grid=(height // step,), in_specs=[pl.BlockS...  12.2 us
  transfers between devices with their start and end apart: 20, of which 6 were waited for; matrix products, arithmetic and copies ran while one was open for 2% of the time, Pallas kernels for 59%

profile of v1, /device:TPU:0, one launch (start us, length us, event | category | flops | bytes accessed | tf_op | source)
XLA Modules:
  0.0 483.2 jit_solution(4510583675458665109)
XLA Ops:
  1.2 6.9 %all-to-all-start = ((f32[8,64,2048]{2,1,0:T(8,128)}), f32[8,64,2048]{2,1,0:T(8,128)}, u32[]{:S(2)}, u32[]{:S(2)}) async-start(f32[8,64,2048]{2,1,0:T(8,128)} %bitcast.24), calls=%async_computation | async-start | bytes 8388608 | tf_op jit(solution)/shard_map/all_to_all | solution.py:534
  17.6 16.0 %width_table.1 = (bf16[2048,2048]{1,0:T(8,128)(2,1)}, bf16[2048,2048]{1,0:T(8,128)(2,1)}) custom-call(s32[1]{0:T(128)} %bitcast.2.place_ref, f32[32,4096]{1,0:T(8,128)} %constant.31.clone.coarse_real, f32[32,4096]{1,0:T(8,128)} %constant.32.clone.coarse_imag, f32[64,4096]{1,0:T(8,128)} %constant.33.clone.fine_real, f32[64,4096]{1,0:T(8,128)} %constant.34.clone.fine_imag), custom_call_target="tpu_custom_call" | custom-call | flops 41943040 | bytes 16777216 | tf_op jit(solution)/shard_map/width_table/pallas_call | solution.py:215
  36.8 17.8 %width_forward.6.refs_3_ = f32[2,2048,1024]{2,1,0:T(8,128)} custom-call(f32[512,2048]{1,0:T(8,128)S(1)} %bitcast.30, bf16[2048,2048]{1,0:T(8,128)(2,1)} %get-tuple-element.24.refs_1_.refs_2_.table_high, bf16[2048,2048]{1,0:T(8,128)(2,1)} %get-tuple-element.25.refs_2_.refs_3_.table_low), custom_call_target="tpu_custom_call" | custom-call | flops 12884901888 | bytes 25165824 | tf_op jit(solution)/shard_map/width_forward/pallas_call | solution.py:256
  54.6 6.5 %collective-permute-done.4.refs_0_ = f32[128,2048]{1,0:T(8,128)S(1)} collective-permute-done((f32[128,2048]{1,0:T(8,128)}, f32[128,2048]{1,0:T(8,128)S(1)}, u32[]{:S(2)}, u32[]{:S(2)}) %collective-permute-start.4) | collective-permute-done | bytes 1048608 | tf_op jit(solution)/shard_map/ppermute | solution.py:519
  61.1 22.5 %collective-permute-done.2.refs_0_ = f32[128,2048]{1,0:T(8,128)S(1)} collective-permute-done((f32[128,2048]{1,0:T(8,128)}, f32[128,2048]{1,0:T(8,128)S(1)}, u32[]{:S(2)}, u32[]{:S(2)}) %collective-permute-start.2) | collective-permute-done | bytes 1048608 | tf_op jit(solution)/shard_map/ppermute | solution.py:519
  83.5 21.7 %collective-permute-done.refs_0_ = f32[128,2048]{1,0:T(8,128)S(1)} collective-permute-done((f32[128,2048]{1,0:T(8,128)}, f32[128,2048]{1,0:T(8,128)S(1)}, u32[]{:S(2)}, u32[]{:S(2)}) %collective-permute-start) | collective-permute-done | bytes 1048608 | tf_op jit(solution)/shard_map/ppermute | solution.py:519
  105.3 19.0 %width_forward.7.refs_4_ = f32[2,2048,1024]{2,1,0:T(8,128)} custom-call(f32[512,2048]{1,0:T(8,128)} %collective-permute-done.8.refs_0_, bf16[2048,2048]{1,0:T(8,128)(2,1)} %get-tuple-element.24.refs_1_.refs_2_.table_high, bf16[2048,2048]{1,0:T(8,128)(2,1)} %get-tuple-element.25.refs_2_.refs_3_.table_low, ...), custom_call_target="tpu_custom_call", output_to_operand_aliasing={{}: (3, {})} | custom-call | flops 12884901888 | bytes 25165824 | tf_op jit(solution)/shard_map/width_forward/pallas_call | solution.py:256
  124.3 13.3 %width_forward.8.refs_4_ = f32[2,2048,1024]{2,1,0:T(8,128)} custom-call(f32[128,2048]{1,0:T(8,128)} %collective-permute-done.6.refs_0_, f32[128,2048]{1,0:T(8,128)S(1)} %collective-permute-done.7.refs_1_, bf16[2048,2048]{1,0:T(8,128)(2,1)} %get-tuple-element.24.refs_1_.refs_2_.table_high, ...), custom_call_target="tpu_custom_call", output_to_operand_aliasing={{}: (4, {})} | custom-call | flops 6442450944 | bytes 20971520 | tf_op jit(solution)/shard_map/width_forward/pallas_call | solution.py:256
  137.6 12.9 %width_forward.9.refs_4_ = f32[2,2048,1024]{2,1,0:T(8,128)} custom-call(f32[128,2048]{1,0:T(8,128)S(1)} %collective-permute-done.4.refs_0_, f32[128,2048]{1,0:T(8,128)S(1)} %collective-permute-done.5.refs_1_, bf16[2048,2048]{1,0:T(8,128)(2,1)} %get-tuple-element.24.refs_1_.refs_2_.table_high, ...), custom_call_target="tpu_custom_call", output_to_operand_aliasing={{}: (4, {})} | custom-call | flops 6442450944 | bytes 20971520 | tf_op jit(solution)/shard_map/width_forward/pallas_call | solution.py:256
  150.5 13.0 %width_forward.10.refs_4_ = f32[2,2048,1024]{2,1,0:T(8,128)} custom-call(f32[128,2048]{1,0:T(8,128)S(1)} %collective-permute-done.2.refs_0_, f32[128,2048]{1,0:T(8,128)S(1)} %collective-permute-done.3.refs_1_, bf16[2048,2048]{1,0:T(8,128)(2,1)} %get-tuple-element.24.refs_1_.refs_2_.table_high, ...), custom_call_target="tpu_custom_call", output_to_operand_aliasing={{}: (4, {})} | custom-call | flops 6442450944 | bytes 20971520 | tf_op jit(solution)/shard_map/width_forward/pallas_call | solution.py:256
  163.5 13.0 %width_forward.11.planes_ref = f32[2,2048,1024]{2,1,0:T(8,128)} custom-call(f32[128,2048]{1,0:T(8,128)S(1)} %collective-permute-done.refs_0_, f32[128,2048]{1,0:T(8,128)S(1)} %collective-permute-done.1.refs_1_, bf16[2048,2048]{1,0:T(8,128)(2,1)} %get-tuple-element.24.refs_1_.refs_2_.table_high, ...), custom_call_target="tpu_custom_call", output_to_operand_aliasing={{}: (4, {})} | custom-call | flops 6442450944 | bytes 20971520 | tf_op jit(solution)/shard_map/width_forward/pallas_call | solution.py:256
  176.4 7.5 %prior_term.1.refs_6_ = f32[8,64,2048]{2,1,0:T(8,128)} custom-call(f32[8,8]{1,0:T(8,128)} %convolution_add_fusion.gram_ref, f32[8,64,2048]{2,1,0:T(8,128)} %all-to-all-done.cube_ref), custom_call_target="tpu_custom_call" | custom-call | flops 16777216 | bytes 8388608 | tf_op jit(solution)/shard_map/prior_term/pallas_call | solution.py:342
  183.9 5.7 %all-to-all-start.1 = ((f32[8,64,2048]{2,1,0:T(8,128)}), f32[8,64,2048]{2,1,0:T(8,128)}, u32[]{:S(2)}, u32[]{:S(2)}) async-start(f32[8,64,2048]{2,1,0:T(8,128)} %prior_term.1.refs_6_), calls=%async_computation.1 | async-start | bytes 8388608 | tf_op jit(solution)/shard_map/all_to_all | solution.py:581
  189.6 79.7 %row_pass.1.planes_ref._ = f32[2,2048,1024]{2,1,0:T(8,128)} custom-call(s32[16]{0:T(128)} %reshape.36.slot_ref, f32[2,2048,1024]{2,1,0:T(8,128)} %width_forward.11.planes_ref, f32[4096,1024]{1,0:T(8,128)} %bitcast.37, f32[4096,1024]{1,0:T(8,128)} %bitcast.38, bf16[32,256,256]{2,1,0:T(8,128)(2,1)} %constant.35.clone.refs_2_, ...), custom_call_target="tpu_custom_call" | custom-call | flops 25769803776 | bytes 67108864 | tf_op jit(solution)/shard_map/row_pass/pallas_call | solution.py:183
  269.3 12.7 %width_back.6 = (f32[128,2048]{1,0:T(8,128)S(1)}, f32[128,2048]{1,0:T(8,128)S(1)}) custom-call(f32[2,2048,1024]{2,1,0:T(8,128)} %row_pass.1.planes_ref._, bf16[2048,2048]{1,0:T(8,128)(2,1)} %get-tuple-element.24.refs_1_.refs_2_.table_high, bf16[2048,2048]{1,0:T(8,128)(2,1)} %get-tuple-element.25.refs_2_.refs_3_.table_low, f32[2,2048,1024]{2,1,0:T(8,128)} %row_pass.1.planes_ref._), custom_call_target="tpu_custom_call" | custom-call | flops 6442450944 | bytes 20971520 | tf_op jit(solution)/shard_map/width_back/pallas_call | solution.py:308
  282.0 12.7 %width_back.7 = (f32[128,2048]{1,0:T(8,128)S(1)}, f32[128,2048]{1,0:T(8,128)S(1)}) custom-call(f32[2,2048,1024]{2,1,0:T(8,128)} %row_pass.1.planes_ref._, bf16[2048,2048]{1,0:T(8,128)(2,1)} %get-tuple-element.24.refs_1_.refs_2_.table_high, bf16[2048,2048]{1,0:T(8,128)(2,1)} %get-tuple-element.25.refs_2_.refs_3_.table_low, f32[128,2048]{1,0:T(8,128)S(1)} %get-tuple-element.26._), custom_call_target="tpu_custom_call" | custom-call | flops 6442450944 | bytes 20971520 | tf_op jit(solution)/shard_map/width_back/pallas_call | solution.py:308
  294.7 12.7 %width_back.8 = (f32[128,2048]{1,0:T(8,128)S(1)}, f32[128,2048]{1,0:T(8,128)S(1)}) custom-call(f32[2,2048,1024]{2,1,0:T(8,128)} %row_pass.1.planes_ref._, bf16[2048,2048]{1,0:T(8,128)(2,1)} %get-tuple-element.24.refs_1_.refs_2_.table_high, bf16[2048,2048]{1,0:T(8,128)(2,1)} %get-tuple-element.25.refs_2_.refs_3_.table_low, f32[128,2048]{1,0:T(8,128)S(1)} %get-tuple-element.27._), custom_call_target="tpu_custom_call" | custom-call | flops 6442450944 | bytes 20971520 | tf_op jit(solution)/shard_map/width_back/pallas_call | solution.py:308
  307.4 12.7 %width_back.9 = (f32[128,2048]{1,0:T(8,128)S(1)}, f32[128,2048]{1,0:T(8,128)S(1)}) custom-call(f32[2,2048,1024]{2,1,0:T(8,128)} %row_pass.1.planes_ref._, bf16[2048,2048]{1,0:T(8,128)(2,1)} %get-tuple-element.24.refs_1_.refs_2_.table_high, bf16[2048,2048]{1,0:T(8,128)(2,1)} %get-tuple-element.25.refs_2_.refs_3_.table_low, f32[128,2048]{1,0:T(8,128)S(1)} %get-tuple-element.28._), custom_call_target="tpu_custom_call" | custom-call | flops 6442450944 | bytes 20971520 | tf_op jit(solution)/shard_map/width_back/pallas_call | solution.py:308
  320.0 18.6 %width_back.10._ = f32[512,2048]{1,0:T(8,128)S(1)} custom-call(f32[2,2048,1024]{2,1,0:T(8,128)} %row_pass.1.planes_ref._, bf16[2048,2048]{1,0:T(8,128)(2,1)} %get-tuple-element.24.refs_1_.refs_2_.table_high, bf16[2048,2048]{1,0:T(8,128)(2,1)} %get-tuple-element.25.refs_2_.refs_3_.table_low, f32[128,2048]{1,0:T(8,128)S(1)} %get-tuple-element.29._), custom_call_target="tpu_custom_call" | custom-call | flops 12884901888 | bytes 25165824 | tf_op jit(solution)/shard_map/width_back/pallas_call | solution.py:308
  340.0 5.8 %collective-permute-done.16 = f32[128,2048]{1,0:T(8,128)S(1)} collective-permute-done((f32[128,2048]{1,0:T(8,128)S(1)}, f32[128,2048]{1,0:T(8,128)S(1)}, u32[]{:S(2)}, u32[]{:S(2)}) %collective-permute-start.16) | collective-permute-done | bytes 1048608 | tf_op jit(solution)/shard_map/ppermute | solution.py:519
  354.7 18.4 %width_back.11.refs_0_ = f32[512,2048]{1,0:T(8,128)S(1)} custom-call(f32[2,2048,1024]{2,1,0:T(8,128)} %row_pass.1.planes_ref._, bf16[2048,2048]{1,0:T(8,128)(2,1)} %get-tuple-element.24.refs_1_.refs_2_.table_high, bf16[2048,2048]{1,0:T(8,128)(2,1)} %get-tuple-element.25.refs_2_.refs_3_.table_low, f32[512,2048]{1,0:T(8,128)} %copy-done.4), custom_call_target="tpu_custom_call" | custom-call | flops 12884901888 | bytes 25165824 | tf_op jit(solution)/shard_map/width_back/pallas_call | solution.py:308
  375.1 63.7 %collective-permute-done.11.refs_3_ = f32[128,2048]{1,0:T(8,128)S(1)} collective-permute-done((f32[128,2048]{1,0:T(8,128)S(1)}, f32[128,2048]{1,0:T(8,128)S(1)}, u32[]{:S(2)}, u32[]{:S(2)}) %collective-permute-start.11) | collective-permute-done | bytes 1048608 | tf_op jit(solution)/shard_map/ppermute | solution.py:519
  456.9 13.8 %reduce_moments.1.sum_ref = f32[4,8,128]{2,1,0:T(8,128)} custom-call(f32[4,8,128]{2,1,0:T(8,128)} %get-tuple-element.31.refs_0_, f32[4,8,128]{2,1,0:T(8,128)} %get-tuple-element.34.refs_1_, f32[4,8,128]{2,1,0:T(8,128)} %get-tuple-element.37.refs_2_, f32[4,8,128]{2,1,0:T(8,128)} %get-tuple-element.40.refs_3_), custom_call_target="tpu_custom_call" | custom-call | tf_op jit(solution)/shard_map/reduce_moments/pallas_call | solution.py:467
  470.8 12.2 %update.1 = (f32[512,2048]{1,0:T(8,128)}, f32[512,2048]{1,0:T(8,128)}, f32[512,2048]{1,0:T(8,128)}) custom-call(f32[4,8,128]{2,1,0:T(8,128)} %reduce_moments.1.sum_ref, f32[512,2048]{1,0:T(8,128)} %bitcast.36, f32[512,2048]{1,0:T(8,128)} %bitcast.35, f32[512,2048]{1,0:T(8,128)} %bitcast.29, f32[512,2048]{1,0:T(8,128)} %get-tuple-element.41.applied_ref), custom_call_target="tpu_custom_call" | custom-call | flops 6291456 | bytes 29360128 | tf_op jit(solution)/shard_map/update/pallas_call | solution.py:504
  (68 shorter events, 43.6 us)
Async XLA Ops:
  0.6 33.0 %copy-start = (f32[8,8]{1,0:T(8,128)S(1)}, f32[8,8]{1,0:T(8,128)}, u32[]{:S(2)}) copy-start(f32[8,8]{1,0:T(8,128)} %param.19) | copy-start | bytes 772
  0.6 104.6 %collective-permute-start.8 = (f32[512,2048]{1,0:T(8,128)}, f32[512,2048]{1,0:T(8,128)}, u32[]{:S(2)}, u32[]{:S(2)}) collective-permute-start(f32[512,2048]{1,0:T(8,128)} %bitcast.23), channel_id=1, source_target_pairs={{0,1},{1,0},{2,3},{3,2},{4,5},{5,4},{6,7},{7,6},{8,9},{9,8},{10,11... | collective-permute-start | bytes 12582920 | tf_op jit(solution)/shard_map/ppermute | solution.py:519
  1.2 175.3 %all-to-all-start = ((f32[8,64,2048]{2,1,0:T(8,128)}), f32[8,64,2048]{2,1,0:T(8,128)}, u32[]{:S(2)}, u32[]{:S(2)}) async-start(f32[8,64,2048]{2,1,0:T(8,128)} %bitcast.24), calls=%async_computation | async-start | bytes 8388608 | tf_op jit(solution)/shard_map/all_to_all | solution.py:534
  8.0 25.6 %copy-start.9 = (s32[8]{0:T(128)S(1)}, s32[8]{0:T(128)}, u32[]{:S(2)}) copy-start(s32[8]{0:T(128)} %param.20) | copy-start | bytes 100
  12.4 42.2 %collective-permute-start.6 = (f32[128,2048]{1,0:T(8,128)}, f32[128,2048]{1,0:T(8,128)}, u32[]{:S(2)}, u32[]{:S(2)}) collective-permute-start(f32[128,2048]{1,0:T(8,128)} %get-tuple-element.45), channel_id=1, source_target_pairs={{0,2},{1,3},{2,0},{3,1},{4,6},{5,7},{6,4},{7,5},{8,10},{9,11},{10,... | collective-permute-start | bytes 3145736 | tf_op jit(solution)/shard_map/ppermute | solution.py:519
  13.9 47.2 %collective-permute-start.4 = (f32[128,2048]{1,0:T(8,128)}, f32[128,2048]{1,0:T(8,128)S(1)}, u32[]{:S(2)}, u32[]{:S(2)}) collective-permute-start(f32[128,2048]{1,0:T(8,128)} %get-tuple-element.46), channel_id=1, source_target_pairs={{0,2},{1,3},{2,0},{3,1},{4,6},{5,7},{6,4},{7,5},{8,10},{9,11},{10,... | collective-permute-start | bytes 3145736 | tf_op jit(solution)/shard_map/ppermute | solution.py:519
  14.4 69.1 %collective-permute-start.2 = (f32[128,2048]{1,0:T(8,128)}, f32[128,2048]{1,0:T(8,128)S(1)}, u32[]{:S(2)}, u32[]{:S(2)}) collective-permute-start(f32[128,2048]{1,0:T(8,128)} %get-tuple-element.47), channel_id=1, source_target_pairs={{0,2},{1,3},{2,0},{3,1},{4,6},{5,7},{6,4},{7,5},{8,10},{9,11},{10,... | collective-permute-start | bytes 3145736 | tf_op jit(solution)/shard_map/ppermute | solution.py:519
  15.9 89.4 %collective-permute-start = (f32[128,2048]{1,0:T(8,128)}, f32[128,2048]{1,0:T(8,128)S(1)}, u32[]{:S(2)}, u32[]{:S(2)}) collective-permute-start(f32[128,2048]{1,0:T(8,128)} %get-tuple-element.48), channel_id=1, source_target_pairs={{0,2},{1,3},{2,0},{3,1},{4,6},{5,7},{6,4},{7,5},{8,10},{9,11},{10,... | collective-permute-start | bytes 3145736 | tf_op jit(solution)/shard_map/ppermute | solution.py:519
  54.6 69.8 %collective-permute-start.7 = (f32[128,2048]{1,0:T(8,128)}, f32[128,2048]{1,0:T(8,128)S(1)}, u32[]{:S(2)}, u32[]{:S(2)}) collective-permute-start(f32[128,2048]{1,0:T(8,128)} %collective-permute-done.6.refs_0_), channel_id=1, source_target_pairs={{0,1},{1,0},{2,3},{3,2},{4,5},{5,4},{6,7},{7,6},{8,9},{9,8},{10,11... | collective-permute-start | bytes 3145736 | tf_op jit(solution)/shard_map/ppermute | solution.py:519
  61.0 76.5 %collective-permute-start.5 = (f32[128,2048]{1,0:T(8,128)S(1)}, f32[128,2048]{1,0:T(8,128)S(1)}, u32[]{:S(2)}, u32[]{:S(2)}) collective-permute-start(f32[128,2048]{1,0:T(8,128)S(1)} %collective-permute-done.4.refs_0_), channel_id=1, source_target_pairs={{0,1},{1,0},{2,3},{3,2},{4,5},{5,4},{6,7},{7,6},{8,9},{9,8},{10,11... | collective-permute-start | bytes 3145736 | tf_op jit(solution)/shard_map/ppermute | solution.py:519
  83.5 67.0 %collective-permute-start.3 = (f32[128,2048]{1,0:T(8,128)S(1)}, f32[128,2048]{1,0:T(8,128)S(1)}, u32[]{:S(2)}, u32[]{:S(2)}) collective-permute-start(f32[128,2048]{1,0:T(8,128)S(1)} %collective-permute-done.2.refs_0_), channel_id=1, source_target_pairs={{0,1},{1,0},{2,3},{3,2},{4,5},{5,4},{6,7},{7,6},{8,9},{9,8},{10,11... | collective-permute-start | bytes 3145736 | tf_op jit(solution)/shard_map/ppermute | solution.py:519
  105.3 58.2 %collective-permute-start.1 = (f32[128,2048]{1,0:T(8,128)S(1)}, f32[128,2048]{1,0:T(8,128)S(1)}, u32[]{:S(2)}, u32[]{:S(2)}) collective-permute-start(f32[128,2048]{1,0:T(8,128)S(1)} %collective-permute-done.refs_0_), channel_id=1, source_target_pairs={{0,1},{1,0},{2,3},{3,2},{4,5},{5,4},{6,7},{7,6},{8,9},{9,8},{10,11... | collective-permute-start | bytes 3145736 | tf_op jit(solution)/shard_map/ppermute | solution.py:519
  183.9 255.8 %all-to-all-start.1 = ((f32[8,64,2048]{2,1,0:T(8,128)}), f32[8,64,2048]{2,1,0:T(8,128)}, u32[]{:S(2)}, u32[]{:S(2)}) async-start(f32[8,64,2048]{2,1,0:T(8,128)} %prior_term.1.refs_6_), calls=%async_computation.1 | async-start | bytes 8388608 | tf_op jit(solution)/shard_map/all_to_all | solution.py:581
  338.7 13.8 %copy-start.4 = (f32[512,2048]{1,0:T(8,128)}, f32[512,2048]{1,0:T(8,128)S(1)}, u32[]{:S(2)}) copy-start(f32[512,2048]{1,0:T(8,128)S(1)} %width_back.10._) | copy-start | bytes 12582916
  338.7 101.1 %collective-permute-start.9 = (f32[512,2048]{1,0:T(8,128)S(1)}, f32[512,2048]{1,0:T(8,128)}, u32[]{:S(2)}, u32[]{:S(2)}) collective-permute-start(f32[512,2048]{1,0:T(8,128)S(1)} %width_back.10._), channel_id=1, source_target_pairs={{0,1},{1,0},{2,3},{3,2},{4,5},{5,4},{6,7},{7,6},{8,9},{9,8},{10,11... | collective-permute-start | bytes 12582920 | tf_op jit(solution)/shard_map/ppermute | solution.py:519
  338.9 6.8 %collective-permute-start.16 = (f32[128,2048]{1,0:T(8,128)S(1)}, f32[128,2048]{1,0:T(8,128)S(1)}, u32[]{:S(2)}, u32[]{:S(2)}) collective-permute-start(f32[128,2048]{1,0:T(8,128)S(1)} %get-tuple-element.38), channel_id=1, source_target_pairs={{0,1},{1,0},{2,3},{3,2},{4,5},{5,4},{6,7},{7,6},{8,9},{9,8},{10,11... | collective-permute-start | bytes 3145736 | tf_op jit(solution)/shard_map/ppermute | solution.py:519
  339.2 9.5 %collective-permute-start.14 = (f32[128,2048]{1,0:T(8,128)S(1)}, f32[128,2048]{1,0:T(8,128)S(1)}, u32[]{:S(2)}, u32[]{:S(2)}) collective-permute-start(f32[128,2048]{1,0:T(8,128)S(1)} %get-tuple-element.35), channel_id=1, source_target_pairs={{0,1},{1,0},{2,3},{3,2},{4,5},{5,4},{6,7},{7,6},{8,9},{9,8},{10,11... | collective-permute-start | bytes 3145736 | tf_op jit(solution)/shard_map/ppermute | solution.py:519
  339.4 11.9 %collective-permute-start.12 = (f32[128,2048]{1,0:T(8,128)S(1)}, f32[128,2048]{1,0:T(8,128)S(1)}, u32[]{:S(2)}, u32[]{:S(2)}) collective-permute-start(f32[128,2048]{1,0:T(8,128)S(1)} %get-tuple-element.32), channel_id=1, source_target_pairs={{0,1},{1,0},{2,3},{3,2},{4,5},{5,4},{6,7},{7,6},{8,9},{9,8},{10,11... | collective-permute-start | bytes 3145736 | tf_op jit(solution)/shard_map/ppermute | solution.py:519
  339.8 13.2 %collective-permute-start.10 = (f32[128,2048]{1,0:T(8,128)S(1)}, f32[128,2048]{1,0:T(8,128)S(1)}, u32[]{:S(2)}, u32[]{:S(2)}) collective-permute-start(f32[128,2048]{1,0:T(8,128)S(1)} %get-tuple-element.30), channel_id=1, source_target_pairs={{0,1},{1,0},{2,3},{3,2},{4,5},{5,4},{6,7},{7,6},{8,9},{9,8},{10,11... | collective-permute-start | bytes 3145736 | tf_op jit(solution)/shard_map/ppermute | solution.py:519
  345.9 106.3 %collective-permute-start.17 = (f32[128,2048]{1,0:T(8,128)S(1)}, f32[128,2048]{1,0:T(8,128)S(1)}, u32[]{:S(2)}, u32[]{:S(2)}) collective-permute-start(f32[128,2048]{1,0:T(8,128)S(1)} %add.30), channel_id=1, source_target_pairs={{0,2},{1,3},{2,0},{3,1},{4,6},{5,7},{6,4},{7,5},{8,10},{9,11},{10,... | collective-permute-start | bytes 3145736 | tf_op jit(solution)/shard_map/ppermute | solution.py:519
  349.9 97.5 %collective-permute-start.15 = (f32[128,2048]{1,0:T(8,128)}, f32[128,2048]{1,0:T(8,128)S(1)}, u32[]{:S(2)}, u32[]{:S(2)}) collective-permute-start(f32[128,2048]{1,0:T(8,128)} %add.29), channel_id=1, source_target_pairs={{0,2},{1,3},{2,0},{3,1},{4,6},{5,7},{6,4},{7,5},{8,10},{9,11},{10,... | collective-permute-start | bytes 3145736 | tf_op jit(solution)/shard_map/ppermute | solution.py:519
  352.5 91.1 %collective-permute-start.13 = (f32[128,2048]{1,0:T(8,128)}, f32[128,2048]{1,0:T(8,128)}, u32[]{:S(2)}, u32[]{:S(2)}) collective-permute-start(f32[128,2048]{1,0:T(8,128)} %add.28), channel_id=1, source_target_pairs={{0,2},{1,3},{2,0},{3,1},{4,6},{5,7},{6,4},{7,5},{8,10},{9,11},{10,... | collective-permute-start | bytes 3145736 | tf_op jit(solution)/shard_map/ppermute | solution.py:519
  353.1 85.7 %collective-permute-start.11 = (f32[128,2048]{1,0:T(8,128)S(1)}, f32[128,2048]{1,0:T(8,128)S(1)}, u32[]{:S(2)}, u32[]{:S(2)}) collective-permute-start(f32[128,2048]{1,0:T(8,128)S(1)} %add.27), channel_id=1, source_target_pairs={{0,2},{1,3},{2,0},{3,1},{4,6},{5,7},{6,4},{7,5},{8,10},{9,11},{10,... | collective-permute-start | bytes 3145736 | tf_op jit(solution)/shard_map/ppermute | solution.py:519
  470.8 12.3 %copy-start.1 = (f32[8,8]{1,0:T(8,128)S(1)}, f32[8,8]{1,0:T(8,128)}, u32[]{:S(2)}) copy-start(f32[8,8]{1,0:T(8,128)} %param.19) | copy-start | bytes 772
  (6 other events, 15.5 us)

commit v2 on v1

--- a/solution.py
+++ b/solution.py
@@ -19,6 +19,7 @@
 PRIOR_FLOOR = 0.25
 HALF = math.sqrt(0.5)
 MESH = pl.DeviceIdType.MESH
+SMALL = pl.CostEstimate(flops=1, bytes_accessed=1, transcendentals=0)
 
 
 def np_split(table):
@@ -111,7 +112,7 @@
 def row_kernel(slot_ref, planes_ref, *refs):
     lanes = planes_ref.shape[2] // LANES
     spectra = refs[:lanes]
-    forward_high, forward_low, inverse_high, inverse_low, _, out_ref, work = refs[lanes:]
+    forward_high, forward_low, inverse_high, inverse_low, out_ref, work = refs[lanes:]
     used = RADIX // 2
     slots = [slot_ref[a] * FINE for a in range(used)]
     steps = FINE // 8 * lanes
@@ -168,7 +169,7 @@
     lax.fori_loop(0, steps, inverse, 0)
 
 
-def row_pass(planes, spectrum, slots, after):
+def row_pass(planes, spectrum, slots):
     _, height, columns = planes.shape
     tables = [jnp.asarray(table) for table in row_tables()]
     lanes = TILE // LANES
@@ -185,26 +186,27 @@
         grid_spec=pltpu.PrefetchScalarGridSpec(
             num_scalar_prefetch=1,
             grid=(columns // TILE,),
-            in_specs=[tile] + strips + [whole] * 4 + [pl.BlockSpec(memory_space=pl.ANY)],
+            in_specs=[tile] + strips + [whole] * 4,
             out_specs=tile,
             scratch_shapes=[pltpu.VMEM((RADIX, 2 * FINE, TILE), jnp.float32)],
         ),
         out_shape=jax.ShapeDtypeStruct(planes.shape, jnp.float32),
         compiler_params=pltpu.CompilerParams(vmem_limit_bytes=60 << 20),
-        cost_estimate=pl.CostEstimate(
-            flops=6 * 2 * 256 * RADIX * 256 * columns, bytes_accessed=64 << 20, transcendentals=0
-        ),
+        cost_estimate=SMALL,
         name="row_pass",
-    )(slots, planes, *([spectrum] * lanes), *tables, after)
+    )(slots, planes, *([spectrum] * lanes), *tables)
 
 
 def table_kernel(place_ref, coarse_real, coarse_imag, fine_real, fine_imag, high_ref, low_ref):
     columns = fine_real.shape[1]
     row = pl.ds(pl.program_id(0) % 8, 1)
-    cr, ci = coarse_real[row, :], coarse_imag[row, :]
-    fr, fi = fine_real[...], fine_imag[...]
-    high_ref[:, :columns], low_ref[:, :columns] = split(cr * fr - ci * fi)
-    high_ref[:, columns:], low_ref[:, columns:] = split(cr * fi + ci * fr)
+    coarse_r, coarse_i = coarse_real[row, :], coarse_imag[row, :]
+    for at in range(0, columns, LANES):
+        real, imag = slice(at, at + LANES), slice(columns + at, columns + at + LANES)
+        cr, ci = coarse_r[:, real], coarse_i[:, real]
+        fr, fi = fine_real[:, real], fine_imag[:, real]
+        high_ref[:, real], low_ref[:, real] = split(cr * fr - ci * fi)
+        high_ref[:, imag], low_ref[:, imag] = split(cr * fi + ci * fr)
 
 
 def width_table(width, columns, length, place):
@@ -221,9 +223,7 @@
             out_specs=[out, out],
         ),
         out_shape=[jax.ShapeDtypeStruct((width, 2 * columns), jnp.bfloat16)] * 2,
-        cost_estimate=pl.CostEstimate(
-            flops=20 * width * columns, bytes_accessed=8 * width * columns, transcendentals=0
-        ),
+        cost_estimate=SMALL,
         name="width_table",
     )(place.reshape(1), *factors)
 
@@ -266,18 +266,14 @@
         scratch_shapes=[pltpu.VMEM((total, width), jnp.bfloat16)] * 2,
         input_output_aliases={len(blocks) + 2: 0} if before else {},
         compiler_params=pltpu.CompilerParams(vmem_limit_bytes=48 << 20),
-        cost_estimate=pl.CostEstimate(
-            flops=12 * total * width * columns,
-            bytes_accessed=8 * width * columns + 4 * total * (width + 2 * columns),
-            transcendentals=0,
-        ),
+        cost_estimate=SMALL,
         name="width_forward",
     )(*blocks, *tables, *before)
 
 
-def back_kernel(count, planes_ref, table_high, table_low, _, *refs):
-    outs = refs[:count]
-    high_ref, low_ref = refs[count:]
+def back_kernel(count, planes_ref, table_high, table_low, *refs):
+    outs = refs[-count - 2 : -2]
+    high_ref, low_ref = refs[-2:]
     columns = planes_ref.shape[2]
 
     @pl.when(pl.program_id(0) == 0)
@@ -312,44 +308,47 @@
             pl.BlockSpec((2, total, columns), lambda n: (0, first // total, 0)),
             table,
             table,
-            pl.BlockSpec(memory_space=pl.ANY),
-        ],
+        ]
+        + [pl.BlockSpec(memory_space=pl.ANY)] * len(after),
         out_specs=[pl.BlockSpec((rows, TILE), lambda n: (0, n)) for rows in sizes],
         out_shape=[jax.ShapeDtypeStruct((rows, width), jnp.float32) for rows in sizes],
         scratch_shapes=[pltpu.VMEM((total, 2 * columns), jnp.bfloat16)] * 2,
         compiler_params=pltpu.CompilerParams(vmem_limit_bytes=48 << 20),
-        cost_estimate=pl.CostEstimate(
-            flops=12 * total * width * columns,
-            bytes_accessed=8 * width * columns + 4 * total * (width + 2 * columns),
-            transcendentals=0,
-        ),
+        cost_estimate=SMALL,
         name="width_back",
-    )(planes, *tables, after)
-
-
-def prior_kernel(gram_ref, cube_ref, out_ref):
-    count = cube_ref.shape[0]
-    for c in range(count):
-        total = gram_ref[c, 0] * cube_ref[0]
-        for k in range(1, count):
-            total = total + gram_ref[c, k] * cube_ref[k]
-        out_ref[c] = total
-
-
-def prior_term(cube, gram):
+    )(planes, *tables, *after)
+
+
+def prior_kernel(gram_ref, cube_ref, _, out_ref):
+    count, rows, width = cube_ref.shape
+    gram = [[gram_ref[c, k] for k in range(count)] for c in range(count)]
+    for at in range(0, rows, 8):
+        for col in range(0, width, LANES):
+            here = slice(at, at + 8), slice(col, col + LANES)
+            values = [cube_ref[(k,) + here] for k in range(count)]
+            for c in range(count):
+                total = gram[c][0] * values[0]
+                for k in range(1, count):
+                    total = total + gram[c][k] * values[k]
+                out_ref[(c,) + here] = total
+
+
+def prior_term(cube, gram, after):
     count, rows, width = cube.shape
     block = pl.BlockSpec((count, 8, width), lambda i: (0, i, 0))
     return pl.pallas_call(
         prior_kernel,
         grid=(rows // 8,),
-        in_specs=[pl.BlockSpec(memory_space=pltpu.SMEM), block],
+        in_specs=[
+            pl.BlockSpec(memory_space=pltpu.SMEM),
+            block,
+            pl.BlockSpec(memory_space=pl.ANY),
+        ],
         out_specs=block,
         out_shape=jax.ShapeDtypeStruct(cube.shape, jnp.float32),
-        cost_estimate=pl.CostEstimate(
-            flops=2 * count * cube.size, bytes_accessed=8 * cube.size, transcendentals=0
-        ),
+        cost_estimate=SMALL,
         name="prior_term",
-    )(gram, cube)
+    )(gram, cube, after)
 
 
 def moment_kernel(terms, *refs):
@@ -383,20 +382,19 @@
     moment_ref[3] += fold(applied * applied)
 
 
-def moments_of(wide, chunk, residual, direction, applied, first):
-    rows, width = chunk[0].shape
-    step = 64 if rows % 64 == 0 else rows
+def moments_of(wide, prior, chunk, residual, direction, applied, first):
+    rows, width = chunk.shape
+    step = min(64, rows)
     at = first // step
     here = pl.BlockSpec((step, width), lambda i: (at + i, 0))
-    own = pl.BlockSpec((step, width), lambda i: (i, 0))
-    terms = len(wide) + len(chunk)
+    chunk_spec = pl.BlockSpec((step, width), lambda i: (i, 0))
+    terms = len(wide) + 2
     before = [] if applied is None else [applied]
     return pl.pallas_call(
         functools.partial(moment_kernel, terms),
         grid=(rows // step,),
         in_specs=[here] * len(wide)
-        + [own] * len(chunk)
-        + [here, here]
+        + [here, chunk_spec, here, here]
         + [pl.BlockSpec(memory_space=pl.ANY)] * len(before),
         out_specs=[here, pl.BlockSpec((4, 8, LANES), lambda i: (0, 0, 0))],
         out_shape=[
@@ -404,61 +402,56 @@
             jax.ShapeDtypeStruct((4, 8, LANES), jnp.float32),
         ],
         input_output_aliases={terms + 2: 0} if before else {},
-        cost_estimate=pl.CostEstimate(
-            flops=10 * rows * width,
-            bytes_accessed=4 * (terms + 3) * rows * width,
-            transcendentals=0,
-        ),
+        cost_estimate=SMALL,
         name="moments",
-    )(*wide, *chunk, residual, direction, *before)
+    )(*wide, prior, chunk, residual, direction, *before)
+
+
+def group_sum(axes, sizes, total, out_ref, mine, landed, send_sem, recv_sem):
+    slot = 0
+    for axis in range(2):
+        size = sizes[axis]
+        me = lax.axis_index(axes[axis])
+        mine[axis] = total
+        copies = [
+            pltpu.make_async_remote_copy(
+                src_ref=mine.at[axis],
+                dst_ref=landed.at[slot + hop - 1],
+                send_sem=send_sem.at[slot + hop - 1],
+                recv_sem=recv_sem.at[slot + hop - 1],
+                device_id={axes[axis]: lax.rem(me + hop, size)},
+                device_id_type=MESH,
+            )
+            for hop in range(1, size)
+        ]
+        for copy in copies:
+            copy.start()
+        for copy in copies:
+            copy.wait()
+        total = jnp.zeros_like(total)
+        for source in range(size):
+            hop = lax.rem(me - source + size, size)
+            arrived = landed[slot + jnp.maximum(hop, 1) - 1]
+            total = total + jnp.where(hop == 0, mine[axis], arrived)
+        slot += size - 1
+    sums = jnp.sum(jnp.sum(total, axis=2, keepdims=True), axis=1, keepdims=True)
+    out_ref[...] = jnp.broadcast_to(sums, total.shape)
 
 
 def reduce_kernel(axes, sizes, parts, *refs):
     inputs = refs[:parts]
     out_ref, mine, landed, send_sem, recv_sem = refs[parts:]
     barrier = pltpu.get_barrier_semaphore()
-
-    def peers(axis):
-        size = sizes[axis]
+    for axis in range(2):
         me = lax.axis_index(axes[axis])
-        return [lax.rem(me + hop, size) for hop in range(1, size)]
-
-    for axis in range(2):
-        for peer in peers(axis):
+        for hop in range(1, sizes[axis]):
+            peer = lax.rem(me + hop, sizes[axis])
             pl.semaphore_signal(barrier, inc=1, device_id={axes[axis]: peer}, device_id_type=MESH)
     total = inputs[0][...]
     for ref in inputs[1:]:
         total = total + ref[...]
     pl.semaphore_wait(barrier, sizes[0] + sizes[1] - 2)
-    slot = 0
-    for axis in range(2):
-        mine[axis] = total
-        copies = []
-        for hop, peer in enumerate(peers(axis)):
-            copies.append(
-                pltpu.make_async_remote_copy(
-                    src_ref=mine.at[axis],
-                    dst_ref=landed.at[slot + hop],
-                    send_sem=send_sem.at[slot + hop],
-                    recv_sem=recv_sem.at[slot + hop],
-                    device_id={axes[axis]: peer},
-                    device_id_type=MESH,
-                )
-            )
-        for copy in copies:
-            copy.start()
-        for hop, copy in enumerate(copies):
-            copy.wait()
-        me = lax.axis_index(axes[axis])
-        size = sizes[axis]
-        total = jnp.zeros_like(total)
-        for source in range(size):
-            hop = lax.rem(me - source + size, size)
-            got = landed[slot + jnp.maximum(hop, 1) - 1]
-            total = total + jnp.where(hop == 0, mine[axis], got)
-        slot += size - 1
-    sums = jnp.sum(jnp.sum(total, axis=2, keepdims=True), axis=1, keepdims=True)
-    out_ref[...] = jnp.broadcast_to(sums, total.shape)
+    group_sum(axes, sizes, total, out_ref, mine, landed, send_sem, recv_sem)
 
 
 def reduce_moments(moments, axes, sizes):
@@ -476,8 +469,240 @@
             pltpu.SemaphoreType.DMA((slots,)),
         ],
         compiler_params=pltpu.CompilerParams(collective_id=0, has_side_effects=True),
+        cost_estimate=SMALL,
         name="reduce_moments",
     )(*moments)
+
+
+def scatter_kernel(axes, sizes, rows_hbm, high_hbm, low_hbm, prior_hbm, residual_hbm,
+                   direction_hbm, applied_hbm, sums_ref, table_high, table_low, held, high_ref,
+                   low_ref, part, landed, beside, own, near, cross, stream, moment, mine, got,
+                   table_sem, held_sem, stream_sem, out_sem, send_sem, recv_sem, group_send,
+                   group_recv):
+    width = table_high.shape[0]
+    columns = held.shape[3]
+    unit = held.shape[2]
+    height = own.shape[0]
+    chunks = height // FINE
+    tiles = width // TILE
+    place = lax.axis_index("facet")
+    sibling = place + 1 - 2 * lax.rem(place, 2)
+    partner = lax.rem(place + 2, 4)
+
+    def peers(axis):
+        me = lax.axis_index(axes[axis])
+        return [lax.rem(me + hop, sizes[axis]) for hop in range(1, sizes[axis])]
+
+    def table_copies(t):
+        at = pl.ds(pl.multiple_of(t * TILE, TILE), TILE)
+        return [
+            pltpu.make_async_copy(source.at[at], target.at[at], table_sem.at[n, t])
+            for n, (source, target) in enumerate(((high_hbm, table_high), (low_hbm, table_low)))
+        ]
+
+    firsts = [2 * height + unit * c for c in range(chunks)]
+    firsts += [height + unit * h for h in range(height // unit)]
+    firsts += [unit * h for h in range(height // unit)]
+    loads = [
+        pltpu.make_async_copy(
+            rows_hbm.at[:, pl.ds(first, unit)], held.at[u % 2], held_sem.at[u % 2]
+        )
+        for u, first in enumerate(firsts)
+    ]
+
+    barrier = pltpu.get_barrier_semaphore()
+    loads[0].start()
+    for t in range(tiles):
+        for copy in table_copies(t):
+            copy.start()
+    for axis in range(2):
+        for peer in peers(axis):
+            pl.semaphore_signal(barrier, inc=1, device_id={axes[axis]: peer}, device_id_type=MESH)
+
+    def image(u, target):
+        loads[u].wait()
+        if u + 1 < len(loads):
+            loads[u + 1].start()
+        for part_at in range(2):
+            col = slice(part_at * columns, (part_at + 1) * columns)
+            high_ref[:, col], low_ref[:, col] = split(held[u % 2, part_at])
+        wide = (((1,), (1,)), ((), ()))
+        dot = functools.partial(
+            lax.dot_general, dimension_numbers=wide, preferred_element_type=jnp.float32
+        )
+
+        def tile(t, _):
+            if u == 0:
+                for copy in table_copies(t):
+                    copy.wait()
+            at = pl.ds(pl.multiple_of(t * TILE, TILE), TILE)
+            weight = table_high[at, :]
+            high = high_ref[...]
+            target[:, at] = (
+                dot(high, weight) + dot(low_ref[...], weight) + dot(high, table_low[at, :])
+            )
+            return 0
+
+        lax.fori_loop(0, tiles, tile, 0)
+
+    def remote(source, target, slot, device):
+        return pltpu.make_async_remote_copy(
+            src_ref=source,
+            dst_ref=target,
+            send_sem=send_sem.at[slot],
+            recv_sem=recv_sem.at[slot],
+            device_id={"facet": device},
+            device_id_type=MESH,
+        )
+
+    def chunk_rows(c):
+        return pl.ds(c * FINE, FINE)
+
+    paired = [
+        remote(part.at[c, pl.ds(FINE, FINE)], landed.at[c], c, sibling) for c in range(chunks)
+    ]
+    crossing = [
+        remote(part.at[c, pl.ds(0, FINE)], cross.at[chunk_rows(c)], chunks + c, partner)
+        for c in range(chunks)
+    ]
+    halves = height // unit
+    nearby = [
+        remote(
+            beside.at[h], near.at[pl.ds(h * unit, unit)], 2 * chunks + h, sibling
+        )
+        for h in range(halves)
+    ]
+
+    def cross_over(c):
+        paired[c].wait_recv()
+
+        def add(i, _):
+            at = pl.ds(pl.multiple_of(i * 8, 8), 8)
+            part[c, at, :] += landed[c, at, :]
+            return 0
+
+        lax.fori_loop(0, FINE // 8, add, 0)
+        crossing[c].start()
+
+    for c in range(chunks):
+        image(c, part.at[c])
+        if c == 0:
+            pl.semaphore_wait(barrier, sizes[0] + sizes[1] - 2)
+        paired[c].start()
+        if c:
+            cross_over(c - 1)
+    for h in range(halves):
+        image(chunks + h, beside.at[h])
+        if h == 0:
+            cross_over(chunks - 1)
+        nearby[h].start()
+    streams = [
+        [
+            pltpu.make_async_copy(source.at[chunk_rows(c)], stream.at[n], stream_sem.at[n])
+            for n, source in enumerate((prior_hbm, residual_hbm, direction_hbm))
+        ]
+        for c in range(chunks)
+    ]
+    for copy in streams[0]:
+        copy.start()
+    for h in range(halves):
+        image(chunks + halves + h, own.at[pl.ds(h * unit, unit)])
+
+    moment[...] = jnp.zeros_like(moment)
+    for copy in nearby:
+        copy.wait_recv()
+    outs = []
+
+    def fold(total):
+        folded = total[:, :LANES]
+        for at in range(LANES, width, LANES):
+            folded = folded + total[:, at : at + LANES]
+        return folded
+
+    for c in range(chunks):
+        for copy in streams[c]:
+            copy.wait()
+        crossing[c].wait_recv()
+
+        def gather(i, _):
+            at = pl.ds(pl.multiple_of(i * 8, 8), 8)
+            here = pl.ds(pl.multiple_of(c * FINE + i * 8, 8), 8)
+            applied = own[here, :] + near[here, :] + cross[here, :] + stream[0, at, :]
+            own[here, :] = applied
+            residual, direction = stream[1, at, :], stream[2, at, :]
+            moment[0] += fold(residual * residual)
+            moment[1] += fold(direction * applied)
+            moment[2] += fold(residual * applied)
+            moment[3] += fold(applied * applied)
+            return 0
+
+        lax.fori_loop(0, FINE // 8, gather, 0)
+        if c + 1 < chunks:
+            for copy in streams[c + 1]:
+                copy.start()
+        out = pltpu.make_async_copy(
+            own.at[chunk_rows(c)], applied_hbm.at[chunk_rows(c)], out_sem.at[c]
+        )
+        out.start()
+        outs.append(out)
+
+    group_sum(axes, sizes, moment[...], sums_ref, mine, got, group_send, group_recv)
+    for copy in paired + crossing + nearby:
+        copy.wait_send()
+    for out in outs:
+        out.wait()
+
+
+def scatter(rows, tables, prior, residual, direction, sizes):
+    height, width = direction.shape
+    columns = rows.shape[2]
+    unit = 2 * FINE
+    chunks = height // FINE
+    hops = sizes[0] + sizes[1] - 2
+    flights = 2 * chunks + height // unit
+    anywhere = pl.BlockSpec(memory_space=pl.ANY)
+    shape = (4, 8, LANES)
+    whole = pltpu.VMEM((height, width), jnp.float32)
+    dma = pltpu.SemaphoreType.DMA
+    return pl.pallas_call(
+        functools.partial(scatter_kernel, ("chan", "facet"), sizes),
+        in_specs=[anywhere] * 6,
+        out_specs=[anywhere, pl.BlockSpec(memory_space=pltpu.VMEM)],
+        out_shape=[
+            jax.ShapeDtypeStruct((height, width), jnp.float32),
+            jax.ShapeDtypeStruct(shape, jnp.float32),
+        ],
+        scratch_shapes=[
+            pltpu.VMEM((width, 2 * columns), jnp.bfloat16),
+            pltpu.VMEM((width, 2 * columns), jnp.bfloat16),
+            pltpu.VMEM((2, 2, unit, columns), jnp.float32),
+            pltpu.VMEM((unit, 2 * columns), jnp.bfloat16),
+            pltpu.VMEM((unit, 2 * columns), jnp.bfloat16),
+            pltpu.VMEM((chunks, unit, width), jnp.float32),
+            pltpu.VMEM((chunks, FINE, width), jnp.float32),
+            pltpu.VMEM((height // unit, unit, width), jnp.float32),
+            whole,
+            whole,
+            whole,
+            pltpu.VMEM((3, FINE, width), jnp.float32),
+            pltpu.VMEM(shape, jnp.float32),
+            pltpu.VMEM((2,) + shape, jnp.float32),
+            pltpu.VMEM((hops,) + shape, jnp.float32),
+            dma((2, width // TILE)),
+            dma((2,)),
+            dma((3,)),
+            dma((chunks,)),
+            dma((flights,)),
+            dma((flights,)),
+            dma((hops,)),
+            dma((hops,)),
+        ],
+        compiler_params=pltpu.CompilerParams(
+            collective_id=1, has_side_effects=True, vmem_limit_bytes=60 << 20
+        ),
+        cost_estimate=SMALL,
+        name="scatter",
+    )(rows, *tables, prior, residual, direction)
 
 
 def update_kernel(
@@ -507,9 +732,7 @@
         in_specs=[pl.BlockSpec(sums.shape, lambda i: (0, 0, 0))] + [block] * 4,
         out_specs=[block] * 3,
         out_shape=[jax.ShapeDtypeStruct((height, width), jnp.float32)] * 3,
-        cost_estimate=pl.CostEstimate(
-            flops=6 * height * width, bytes_accessed=28 * height * width, transcendentals=0
-        ),
+        cost_estimate=SMALL,
         name="update",
     )(sums, solution, residual, direction, applied)
 
@@ -529,9 +752,23 @@
     own = direction[0]
     top = facets // 2
     per_facet = height // FINE
-
-    stacked = own.reshape(channel_count, height // channel_count, width)
-    regrouped = lax.all_to_all(stacked, "chan", split_axis=0, concat_axis=0, tiled=True)
+    barrier = lax.optimization_barrier
+
+    chunks = [own[at * FINE : (at + 1) * FINE] for at in range(per_facet)]
+    crossed = [swap_pairs(chunk, facets, top) for chunk in chunks]
+
+    def spread(block, key):
+        blocks = {key: block}
+        bit = top // 2
+        while bit:
+            blocks.update({k ^ bit: swap_pairs(blocks[k], facets, bit) for k in list(blocks)})
+            bit //= 2
+        return blocks
+
+    near = spread(own, 0)
+
+    cube = own.reshape(channel_count, height // channel_count, width)
+    regrouped = lax.all_to_all(cube, "chan", split_axis=0, concat_axis=0, tiled=True)
     one_hot = (
         slot_channel[:, None] == jnp.arange(channel_count, dtype=jnp.int32)[None, :]
     ).astype(jnp.float32)
@@ -539,59 +776,56 @@
     gram = jnp.einsum("cq,dq->cd", loadings, loadings, precision=HIGHEST)
     gram = gram + PRIOR_FLOOR * jnp.eye(channel_count, dtype=jnp.float32)
 
-    chunks = [own[at * FINE : (at + 1) * FINE] for at in range(per_facet)]
-    far = []
-    for chunk in chunks:
-        blocks = {top: swap_pairs(chunk, facets, top)}
-        bit = top // 2
-        while bit:
-            blocks.update({key ^ bit: swap_pairs(blocks[key], facets, bit) for key in list(blocks)})
-            bit //= 2
-        far.append(blocks)
-    near = {0: own}
-    bit = top // 2
-    while bit:
-        near.update({key ^ bit: swap_pairs(near[key], facets, bit) for key in list(near)})
-        bit //= 2
-
     groups = []
     if per_facet > 1:
-        groups += [([near[key]], [(key, s) for s in range(per_facet)]) for key in range(top)]
+        groups += [[(key, s) for s in range(per_facet)] for key in range(top)]
     else:
-        groups.append(([near[key] for key in range(top)], [(key, 0) for key in range(top)]))
-    for s, blocks in enumerate(far):
-        keys = range(top, facets)
-        groups.append(([blocks[key] for key in keys], [(key, s) for key in keys]))
-    order = [entry for _, entries in groups for entry in entries]
+        groups.append([(key, 0) for key in range(top)])
+    groups += [[(key, s) for key in range(top, facets)] for s in range(per_facet)]
+    starts = np.cumsum([0] + [len(entries) * FINE for entries in groups])
     slot_of = np.zeros((facets, per_facet), np.int32)
-    for at, (key, s) in enumerate(order):
+    for at, (key, s) in enumerate(entry for entries in groups for entry in entries):
         slot_of[key, s] = at
     slots = jnp.asarray(slot_of)[jnp.arange(facets, dtype=jnp.int32) ^ place].reshape(-1)
 
     tables = width_table(width, columns, length, place)
     planes = None
-    first = 0
-    starts = []
-    for blocks, entries in groups:
-        planes = width_forward(blocks, tables, planes, first, columns, facets * height)
-        starts.append(first)
-        first += len(entries) * FINE
-
-    local_prior = prior_term(regrouped, gram)
-    prior = lax.all_to_all(local_prior, "chan", split_axis=0, concat_axis=0, tiled=True)
-    prior = prior.reshape(height, width)
-
-    rows = row_pass(planes, spectra[0], slots, local_prior)
-
-    after = rows
-    arrived = []
+    far = {}
+    for step, entries in enumerate(groups):
+        if entries[0][0] >= top:
+            blocks = [far[s][key] for key, s in entries]
+        elif per_facet > 1:
+            blocks = [near[entries[0][0]]]
+        else:
+            blocks = [near[key] for key, _ in entries]
+        planes = width_forward(
+            blocks, tables, planes, int(starts[step]), columns, facets * height
+        )
+        if step < per_facet:
+            block, planes = barrier((crossed[step], planes))
+            far[step] = spread(block, top)
+        if step == len(groups) - 2:
+            local = prior_term(regrouped, gram, planes)
+            local, planes = barrier((local, planes))
+            prior = lax.all_to_all(local, "chan", split_axis=0, concat_axis=0, tiled=True)
+            prior = prior.reshape(height, width)
+
+    rows = row_pass(planes, spectra[0], slots)
+
+    sizes = (lax.axis_size("chan"), facets)
+    if facets == 4 and per_facet % 2 == 0:
+        applied, sums = scatter(rows, tables, prior, residual[0], own, sizes)
+        results = update(sums, solution[0], residual[0], own, applied)
+        return tuple(result[None] for result in results)
+
+    arrived = {}
     near_sums = {}
-    for (blocks, entries), start in list(zip(groups, starts))[::-1]:
-        if entries[0][0] < top:
-            continue
-        sizes = [FINE] * len(entries)
-        parts = width_back(rows, tables, start, sizes, after)
-        after = parts[0]
+    held = [rows]
+    previous = None
+    sequence = [at for at in range(len(groups)) if groups[at][0][0] >= top]
+    sequence += [at for at in range(len(groups)) if groups[at][0][0] < top][::-1]
+
+    def send(entries, parts):
         sums = {key: part for (key, _), part in zip(entries, parts)}
         bit = 1
         while bit < top:
@@ -601,17 +835,24 @@
                 if not key & bit
             }
             bit *= 2
-        arrived.append((entries[0][1], swap_pairs(sums[top], facets, top)))
-    for (blocks, entries), start in list(zip(groups, starts))[::-1]:
-        if entries[0][0] >= top:
-            continue
-        if per_facet > 1:
-            key = entries[0][0]
-            near_sums[key] = width_back(rows, tables, start, [height], after)[0]
-            after = near_sums[key]
+        arrived[entries[0][1]] = swap_pairs(sums[top], facets, top)
+        return sums[top]
+
+    for turn_at, at in enumerate(sequence):
+        entries = groups[at]
+        far_rows = entries[0][0] >= top
+        counts = [FINE] * len(entries) if far_rows or per_facet == 1 else [height]
+        parts = width_back(rows, tables, int(starts[at]), counts, held)
+        held = [parts[0]]
+        if previous is not None:
+            held.append(send(*previous))
+            previous = None
+        if turn_at >= 3 and turn_at - 3 < per_facet:
+            held.append(arrived[groups[sequence[turn_at - 3]][0][1]])
+        if far_rows:
+            previous = (entries, parts)
         else:
-            parts = width_back(rows, tables, start, [FINE] * len(entries), after)
-            near_sums = {key: part for (key, _), part in zip(entries, parts)}
+            near_sums.update({key: part for (key, _), part in zip(entries, parts)})
     bit = 1
     while 2 * bit < top:
         near_sums = {
@@ -620,14 +861,16 @@
             if not key & bit
         }
         bit *= 2
-    wide = [near_sums[0], swap_pairs(near_sums[bit], facets, bit), prior]
+    wide = [near_sums[0], swap_pairs(near_sums[bit], facets, bit)]
 
     applied = None
     moments = []
-    for s, part in arrived:
-        applied, moment = moments_of(wide, [part], residual[0], own, applied, s * FINE)
+    for s in range(per_facet):
+        first = s * FINE
+        applied, moment = moments_of(
+            wide, prior, arrived[s], residual[0], own, applied, first
+        )
         moments.append(moment)
-    sizes = (lax.axis_size("chan"), facets)
     sums = reduce_moments(moments, ("chan", "facet"), sizes)
     results = update(sums, solution[0], residual[0], own, applied)
     return tuple(result[None] for result in results)

time: 485 us -> 367 us (0.76)
  waiting for transfers between devices: 122 us -> 6.9 us
  Pallas kernels: 321 us -> 331 us
  starting transfers between devices: 23.6 us -> 18.1 us
  local copies, waits for them, and re-layouts: 12.6 us -> 7.31 us
    ppermute x18 -> x9, waiting for transfers between devices: 122 us -> 6.9 us  [swap_pairs(): return lax.ppermute(array, 'facet', pairs)]
    pallas_call x11 -> x1, Pallas kernels: 117 us -> 126 us  [scatter(): pl.pallas_call(functools.partial(scatter_kernel, ('chan', 'facet'), sizes...]
    ppermute x18 -> x9, starting transfers between devices: 11 us -> 4.66 us  [swap_pairs(): return lax.ppermute(array, 'facet', pairs)]
    unnamed x20 -> x12, local copies, waits for them, and re-layouts: 7.13 us -> 2.22 us
  transfers between devices with their start and end apart: 20 -> 11, of which waited for: 6 -> 2; matrix products, arithmetic and copies ran while one was open for 2% -> 2% of each run, Pallas kernels for 59% -> 51%
where the time goes in v2:
time: 367 us; the launch traced here: 365 us
  Pallas kernels  331 us (90%)
  starting transfers between devices  18.1 us (5%)
  local copies, waits for them, and re-layouts  7.31 us (2%)
  waiting for transfers between devices  6.9 us (2%)
    pallas_call x1, Pallas kernels, scatter(): pl.pallas_call(functools.partial(scatter_kernel, ('chan', 'facet'), sizes...  126 us
    pallas_call x6, Pallas kernels, width_forward(): pl.pallas_call(functools.partial(width_kernel, len(blocks)), grid=(2 * ti...  88.6 us
    pallas_call x1, Pallas kernels, row_pass(): pl.pallas_call(row_kernel, grid_spec=pltpu.PrefetchScalarGridSpec(num_sca...  79.7 us
    pallas_call x1, Pallas kernels, width_table(): pl.pallas_call(table_kernel, grid_spec=pltpu.PrefetchScalarGridSpec(num_s...  17 us
    pallas_call x1, Pallas kernels, update(): pl.pallas_call(update_kernel, grid=(height // step,), in_specs=[pl.BlockS...  12.2 us
    pallas_call x1, Pallas kernels, prior_term(): pl.pallas_call(prior_kernel, grid=(rows // 8,), in_specs=[pl.BlockSpec(me...  7.48 us
  transfers between devices with their start and end apart: 11, of which 2 were waited for; matrix products, arithmetic and copies ran while one was open for 2% of the time, Pallas kernels for 51%

profile of v2, /device:TPU:0, one launch (start us, length us, event | category | flops | bytes accessed | tf_op | source)
XLA Modules:
  0.0 365.3 jit_solution(11928461765976080969)
XLA Ops:
  0.6 7.3 %all-to-all-start = ((f32[8,64,2048]{2,1,0:T(8,128)}), f32[8,64,2048]{2,1,0:T(8,128)}, u32[]{:S(2)}, u32[]{:S(2)}) async-start(f32[8,64,2048]{2,1,0:T(8,128)} %bitcast.23), calls=%async_computation | async-start | bytes 8388608 | tf_op jit(solution)/shard_map/all_to_all | solution.py:771
  8.0 3.9 %slice_bitcast_fusion = (f32[128,2048]{1,0:T(8,128)}, f32[128,2048]{1,0:T(8,128)S(1)}, f32[128,2048]{1,0:T(8,128)}, f32[128,2048]{1,0:T(8,128)}) fusion(f32[1,512,2048]{2,1,0:T(8,128)} %param.17), kind=kLoop, calls=%fused_computation.2 | loop fusion | bytes 8388608 | tf_op jit(solution)/shard_map/slice | solution.py:757
  11.9 1.5 collective-permute-start.3
  13.4 0.5 collective-permute-start.1
  13.9 17.0 %width_table.1 = (bf16[2048,2048]{1,0:T(8,128)(2,1)}, bf16[2048,2048]{1,0:T(8,128)(2,1)}) custom-call(s32[1]{0:T(128)} %bitcast.4.place_ref, f32[32,4096]{1,0:T(8,128)} %constant.31.clone.coarse_real, f32[32,4096]{1,0:T(8,128)} %constant.32.clone.coarse_imag, f32[64,4096]{1,0:T(8,128)} %constant.33.clone.fine_real, f32[64,4096]{1,0:T(8,128)} %constant.34.clone.fine_imag), custom_call_target="tpu_custom_call" | custom-call | flops 1 | bytes 1 | tf_op jit(solution)/shard_map/width_table/pallas_call | solution.py:217
  30.9 2.2 copy-done.2
  33.1 17.9 %width_forward.6.refs_3_ = f32[2,2048,1024]{2,1,0:T(8,128)} custom-call(f32[512,2048]{1,0:T(8,128)S(1)} %bitcast.27, bf16[2048,2048]{1,0:T(8,128)(2,1)} %get-tuple-element.20.refs_1_.refs_2_.high_hbm, bf16[2048,2048]{1,0:T(8,128)(2,1)} %get-tuple-element.21.refs_2_.refs_3_.low_hbm), custom_call_target="tpu_custom_call" | custom-call | flops 1 | bytes 1 | tf_op jit(solution)/shard_map/width_forward/pallas_call | solution.py:256
  50.9 1.6 collective-permute-start.5
  52.5 0.5 collective-permute-start
  53.0 19.0 %width_forward.7.refs_4_ = f32[2,2048,1024]{2,1,0:T(8,128)} custom-call(f32[512,2048]{1,0:T(8,128)} %collective-permute-done.2.refs_0_, bf16[2048,2048]{1,0:T(8,128)(2,1)} %get-tuple-element.20.refs_1_.refs_2_.high_hbm, bf16[2048,2048]{1,0:T(8,128)(2,1)} %get-tuple-element.21.refs_2_.refs_3_.low_hbm, ...), custom_call_target="tpu_custom_call", output_to_operand_aliasing={{}: (3, {})} | custom-call | flops 1 | bytes 1 | tf_op jit(solution)/shard_map/width_forward/pallas_call | solution.py:256
  72.1 13.0 %width_forward.8.refs_4_ = f32[2,2048,1024]{2,1,0:T(8,128)} custom-call(f32[128,2048]{1,0:T(8,128)S(1)} %collective-permute-done.3.refs_0_, f32[128,2048]{1,0:T(8,128)S(1)} %collective-permute-done.6.refs_1_, bf16[2048,2048]{1,0:T(8,128)(2,1)} %get-tuple-element.20.refs_1_.refs_2_.high_hbm, ...), custom_call_target="tpu_custom_call", output_to_operand_aliasing={{}: (4, {})} | custom-call | flops 1 | bytes 1 | tf_op jit(solution)/shard_map/width_forward/pallas_call | solution.py:256
  85.8 0.7 convolution_add_fusion.gram_ref
  86.5 12.9 %width_forward.9.refs_4_ = f32[2,2048,1024]{2,1,0:T(8,128)} custom-call(f32[128,2048]{1,0:T(8,128)S(1)} %collective-permute-done.1.refs_0_, f32[128,2048]{1,0:T(8,128)S(1)} %collective-permute-done.4.refs_1_, bf16[2048,2048]{1,0:T(8,128)(2,1)} %get-tuple-element.20.refs_1_.refs_2_.high_hbm, ...), custom_call_target="tpu_custom_call", output_to_operand_aliasing={{}: (4, {})} | custom-call | flops 1 | bytes 1 | tf_op jit(solution)/shard_map/width_forward/pallas_call | solution.py:256
  99.4 5.4 %collective-permute-done.refs_0_ = f32[128,2048]{1,0:T(8,128)S(1)} collective-permute-done((f32[128,2048]{1,0:T(8,128)S(1)}, f32[128,2048]{1,0:T(8,128)S(1)}, u32[]{:S(2)}, u32[]{:S(2)}) %collective-permute-start) | collective-permute-done | bytes 1048608 | tf_op jit(solution)/shard_map/ppermute | solution.py:742
  104.9 12.9 %width_forward.10._.refs_4_ = f32[2,2048,1024]{2,1,0:T(8,128)} custom-call(f32[128,2048]{1,0:T(8,128)S(1)} %collective-permute-done.5.refs_0_, f32[128,2048]{1,0:T(8,128)S(1)} %collective-permute-done.8.refs_1_, bf16[2048,2048]{1,0:T(8,128)(2,1)} %get-tuple-element.20.refs_1_.refs_2_.high_hbm, ...), custom_call_target="tpu_custom_call", output_to_operand_aliasing={{}: (4, {})} | custom-call | flops 1 | bytes 1 | tf_op jit(solution)/shard_map/width_forward/pallas_call | solution.py:256
  117.8 7.5 %prior_term.1 = f32[8,64,2048]{2,1,0:T(8,128)} custom-call(f32[8,8]{1,0:T(8,128)} %convolution_add_fusion.gram_ref, f32[8,64,2048]{2,1,0:T(8,128)} %all-to-all-done.cube_ref, f32[2,2048,1024]{2,1,0:T(8,128)} %width_forward.10._.refs_4_), custom_call_target="tpu_custom_call" | custom-call | flops 1 | bytes 1 | tf_op jit(solution)/shard_map/prior_term/pallas_call | solution.py:339
  125.3 6.1 %all-to-all-start.1 = ((f32[8,64,2048]{2,1,0:T(8,128)}), f32[8,64,2048]{2,1,0:T(8,128)}, u32[]{:S(2)}, u32[]{:S(2)}) async-start(f32[8,64,2048]{2,1,0:T(8,128)} %prior_term.1), calls=%async_computation.1 | async-start | bytes 8388608 | tf_op jit(solution)/shard_map/all_to_all | solution.py:810
  131.5 0.6 gather_fusion
  132.0 0.6 reshape.36.slot_ref
  132.6 1.5 collective-permute-done.7.refs_1_
  134.1 12.9 %width_forward.11.planes_ref = f32[2,2048,1024]{2,1,0:T(8,128)} custom-call(f32[128,2048]{1,0:T(8,128)S(1)} %collective-permute-done.refs_0_, f32[128,2048]{1,0:T(8,128)S(1)} %collective-permute-done.7.refs_1_, bf16[2048,2048]{1,0:T(8,128)(2,1)} %get-tuple-element.20.refs_1_.refs_2_.high_hbm, ...), custom_call_target="tpu_custom_call", output_to_operand_aliasing={{}: (4, {})} | custom-call | flops 1 | bytes 1 | tf_op jit(solution)/shard_map/width_forward/pallas_call | solution.py:256
  147.0 79.7 %row_pass.1.rows_hbm = f32[2,2048,1024]{2,1,0:T(8,128)} custom-call(s32[16]{0:T(128)} %reshape.36.slot_ref, f32[2,2048,1024]{2,1,0:T(8,128)} %width_forward.11.planes_ref, f32[4096,1024]{1,0:T(8,128)} %bitcast.28, f32[4096,1024]{1,0:T(8,128)} %bitcast.29, bf16[32,256,256]{2,1,0:T(8,128)(2,1)} %constant.35.clone.refs_2_, ...), custom_call_target="tpu_custom_call" | custom-call | flops 1 | bytes 1 | tf_op jit(solution)/shard_map/row_pass/pallas_call | solution.py:184
  226.7 126.3 %scatter.1 = (f32[512,2048]{1,0:T(8,128)}, f32[4,8,128]{2,1,0:T(8,128)}) custom-call(f32[2,2048,1024]{2,1,0:T(8,128)} %row_pass.1.rows_hbm, bf16[2048,2048]{1,0:T(8,128)(2,1)} %get-tuple-element.20.refs_1_.refs_2_.high_hbm, bf16[2048,2048]{1,0:T(8,128)(2,1)} %get-tuple-element.21.refs_2_.refs_3_.low_hbm, f32[512,2048]{1,0:T(8,128)} %bitcast.9.prior_hbm, ...), custom_call_target="tpu_custom_call" | custom-call | flops 1 | bytes 1 | tf_op jit(solution)/shard_map/scatter/pallas_call | solution.py:667
  353.0 12.2 %update.1 = (f32[512,2048]{1,0:T(8,128)}, f32[512,2048]{1,0:T(8,128)}, f32[512,2048]{1,0:T(8,128)}) custom-call(f32[4,8,128]{2,1,0:T(8,128)} %get-tuple-element.32.sum_ref, f32[512,2048]{1,0:T(8,128)} %bitcast.32, f32[512,2048]{1,0:T(8,128)} %bitcast.31, f32[512,2048]{1,0:T(8,128)} %bitcast.26, f32[512,2048]{1,0:T(8,128)} %get-tuple-element.33.applied_ref), custom_call_target="tpu_custom_call" | custom-call | flops 1 | bytes 1 | tf_op jit(solution)/shard_map/update/pallas_call | solution.py:729
  (28 shorter events, 0.8 us)
Async XLA Ops:
  0.6 84.9 %copy-start = (f32[8,8]{1,0:T(8,128)S(1)}, f32[8,8]{1,0:T(8,128)}, u32[]{:S(2)}) copy-start(f32[8,8]{1,0:T(8,128)} %param.19) | copy-start | bytes 772
  0.6 117.2 %all-to-all-start = ((f32[8,64,2048]{2,1,0:T(8,128)}), f32[8,64,2048]{2,1,0:T(8,128)}, u32[]{:S(2)}, u32[]{:S(2)}) async-start(f32[8,64,2048]{2,1,0:T(8,128)} %bitcast.23), calls=%async_computation | async-start | bytes 8388608 | tf_op jit(solution)/shard_map/all_to_all | solution.py:771
  7.9 45.1 %collective-permute-start.2 = (f32[512,2048]{1,0:T(8,128)}, f32[512,2048]{1,0:T(8,128)}, u32[]{:S(2)}, u32[]{:S(2)}) collective-permute-start(f32[512,2048]{1,0:T(8,128)} %bitcast.24), channel_id=1, source_target_pairs={{0,1},{1,0},{2,3},{3,2},{4,5},{5,4},{6,7},{7,6},{8,9},{9,8},{10,11... | collective-permute-start | bytes 12582920 | tf_op jit(solution)/shard_map/ppermute | solution.py:742
  11.9 39.0 %collective-permute-start.3 = (f32[128,2048]{1,0:T(8,128)S(1)}, f32[128,2048]{1,0:T(8,128)S(1)}, u32[]{:S(2)}, u32[]{:S(2)}) collective-permute-start(f32[128,2048]{1,0:T(8,128)S(1)} %get-tuple-element.38), channel_id=1, source_target_pairs={{0,2},{1,3},{2,0},{3,1},{4,6},{5,7},{6,4},{7,5},{8,10},{9,11},{10,... | collective-permute-start | bytes 3145736 | tf_op jit(solution)/shard_map/ppermute | solution.py:742
  13.4 58.7 %collective-permute-start.1 = (f32[128,2048]{1,0:T(8,128)}, f32[128,2048]{1,0:T(8,128)S(1)}, u32[]{:S(2)}, u32[]{:S(2)}) collective-permute-start(f32[128,2048]{1,0:T(8,128)} %get-tuple-element.39), channel_id=1, source_target_pairs={{0,2},{1,3},{2,0},{3,1},{4,6},{5,7},{6,4},{7,5},{8,10},{9,11},{10,... | collective-permute-start | bytes 3145736 | tf_op jit(solution)/shard_map/ppermute | solution.py:742
  30.9 2.2 copy-start.2
  33.1 19.4 %copy-start.3 = (f32[128,2048]{1,0:T(8,128)S(1)}, f32[128,2048]{1,0:T(8,128)}, u32[]{:S(2)}) copy-start(f32[128,2048]{1,0:T(8,128)} %get-tuple-element.40) | copy-start | bytes 3145732
  50.9 21.2 %collective-permute-start.6 = (f32[128,2048]{1,0:T(8,128)S(1)}, f32[128,2048]{1,0:T(8,128)S(1)}, u32[]{:S(2)}, u32[]{:S(2)}) collective-permute-start(f32[128,2048]{1,0:T(8,128)S(1)} %collective-permute-done.3.refs_0_), channel_id=1, source_target_pairs={{0,1},{1,0},{2,3},{3,2},{4,5},{5,4},{6,7},{7,6},{8,9},{9,8},{10,11... | collective-permute-start | bytes 3145736 | tf_op jit(solution)/shard_map/ppermute | solution.py:742
  50.9 34.2 %collective-permute-start.5 = (f32[128,2048]{1,0:T(8,128)}, f32[128,2048]{1,0:T(8,128)S(1)}, u32[]{:S(2)}, u32[]{:S(2)}) collective-permute-start(f32[128,2048]{1,0:T(8,128)} %get-tuple-element.37), channel_id=1, source_target_pairs={{0,2},{1,3},{2,0},{3,1},{4,6},{5,7},{6,4},{7,5},{8,10},{9,11},{10,... | collective-permute-start | bytes 3145736 | tf_op jit(solution)/shard_map/ppermute | solution.py:742
  52.5 52.4 %collective-permute-start = (f32[128,2048]{1,0:T(8,128)S(1)}, f32[128,2048]{1,0:T(8,128)S(1)}, u32[]{:S(2)}, u32[]{:S(2)}) collective-permute-start(f32[128,2048]{1,0:T(8,128)S(1)} %copy-done.3), channel_id=1, source_target_pairs={{0,2},{1,3},{2,0},{3,1},{4,6},{5,7},{6,4},{7,5},{8,10},{9,11},{10,... | collective-permute-start | bytes 3145736 | tf_op jit(solution)/shard_map/ppermute | solution.py:742
  72.0 13.5 %copy-start.5 = (s32[8]{0:T(128)S(1)}, s32[8]{0:T(128)}, u32[]{:S(2)}) copy-start(s32[8]{0:T(128)} %param.20) | copy-start | bytes 100
  72.0 14.5 %collective-permute-start.4 = (f32[128,2048]{1,0:T(8,128)S(1)}, f32[128,2048]{1,0:T(8,128)S(1)}, u32[]{:S(2)}, u32[]{:S(2)}) collective-permute-start(f32[128,2048]{1,0:T(8,128)S(1)} %collective-permute-done.1.refs_0_), channel_id=1, source_target_pairs={{0,1},{1,0},{2,3},{3,2},{4,5},{5,4},{6,7},{7,6},{8,9},{9,8},{10,11... | collective-permute-start | bytes 3145736 | tf_op jit(solution)/shard_map/ppermute | solution.py:742
  85.1 19.8 %collective-permute-start.8 = (f32[128,2048]{1,0:T(8,128)S(1)}, f32[128,2048]{1,0:T(8,128)S(1)}, u32[]{:S(2)}, u32[]{:S(2)}) collective-permute-start(f32[128,2048]{1,0:T(8,128)S(1)} %collective-permute-done.5.refs_0_), channel_id=1, source_target_pairs={{0,1},{1,0},{2,3},{3,2},{4,5},{5,4},{6,7},{7,6},{8,9},{9,8},{10,11... | collective-permute-start | bytes 3145736 | tf_op jit(solution)/shard_map/ppermute | solution.py:742
  125.3 6.2 %copy-start.4 = (s32[4,4]{1,0:T(4,128)S(1)}, s32[4,4]{1,0:T(4,128)}, u32[]{:S(2)}) copy-start(s32[4,4]{1,0:T(4,128)} %constant.30.clone) | copy-start | bytes 196
  125.3 101.4 %all-to-all-start.1 = ((f32[8,64,2048]{2,1,0:T(8,128)}), f32[8,64,2048]{2,1,0:T(8,128)}, u32[]{:S(2)}, u32[]{:S(2)}) async-start(f32[8,64,2048]{2,1,0:T(8,128)} %prior_term.1), calls=%async_computation.1 | async-start | bytes 8388608 | tf_op jit(solution)/shard_map/all_to_all | solution.py:810
  131.4 2.7 collective-permute-start.7
  353.0 12.2 %copy-start.1 = (f32[8,8]{1,0:T(8,128)S(1)}, f32[8,8]{1,0:T(8,128)}, u32[]{:S(2)}) copy-start(f32[8,8]{1,0:T(8,128)} %param.19) | copy-start | bytes 772

commit v3 on v2

--- a/solution.py
+++ b/solution.py
@@ -474,11 +474,269 @@
     )(*moments)
 
 
+def gather_kernel(axes, sizes, basis_ref, slot_ref, own_hbm, coarse_real_hbm, coarse_imag_hbm,
+                  fine_real_hbm, fine_imag_hbm, planes_hbm, prior_hbm, high_hbm, low_hbm,
+                  table_high, table_low, coarse, fine, mine, beside, cross, passed, high_ref,
+                  low_ref, result, cube, gram, own_sem, factor_sem, table_sem, result_sem,
+                  prior_sem, send_sem, recv_sem, group_send, group_recv):
+    height, width = own_hbm.shape
+    columns = fine.shape[2]
+    unit = high_ref.shape[0]
+    chunks = height // FINE
+    halves = height // unit
+    slots = sizes[0]
+    block = height // slots
+    place = lax.axis_index("facet")
+    me = lax.axis_index("chan")
+    sibling = place + 1 - 2 * lax.rem(place, 2)
+    partner = lax.rem(place + 2, 4)
+
+    def chunk_rows(c):
+        return pl.ds(c * FINE, FINE)
+
+    def half_rows(h):
+        return pl.ds(h * unit, unit)
+
+    def block_rows(at):
+        return pl.ds(pl.multiple_of(at * block, block), block)
+
+    def remote(source, target, slot, device):
+        return pltpu.make_async_remote_copy(
+            src_ref=source,
+            dst_ref=target,
+            send_sem=send_sem.at[slot],
+            recv_sem=recv_sem.at[slot],
+            device_id={"facet": device},
+            device_id_type=MESH,
+        )
+
+    crossing = [
+        remote(own_hbm.at[chunk_rows(c)], cross.at[c], c, partner) for c in range(chunks)
+    ]
+    nearby = [
+        remote(own_hbm.at[half_rows(h)], beside.at[half_rows(h)], chunks + h, sibling)
+        for h in range(halves)
+    ]
+    passing = [
+        remote(cross.at[c], passed.at[c], chunks + halves + c, sibling) for c in range(chunks)
+    ]
+    regroup = []
+    for hop in range(1, slots):
+        peer = lax.rem(me + hop, slots)
+        regroup.append(
+            pltpu.make_async_remote_copy(
+                src_ref=own_hbm.at[block_rows(peer)],
+                dst_ref=cube.at[me],
+                send_sem=group_send.at[hop - 1],
+                recv_sem=group_recv.at[hop - 1],
+                device_id={"chan": peer},
+                device_id_type=MESH,
+            )
+        )
+    kept = pltpu.make_async_copy(own_hbm.at[block_rows(me)], cube.at[me], prior_sem.at[0])
+    own_loads = [
+        pltpu.make_async_copy(own_hbm.at[half_rows(h)], mine.at[half_rows(h)], own_sem.at[h])
+        for h in range(halves)
+    ]
+    col = pl.ds(pl.multiple_of(place * columns, columns), columns)
+    factors = [
+        pltpu.make_async_copy(source.at[:, col], target, factor_sem.at[n])
+        for n, (source, target) in enumerate(
+            (
+                (coarse_real_hbm, coarse.at[0]),
+                (coarse_imag_hbm, coarse.at[1]),
+                (fine_real_hbm, fine.at[0]),
+                (fine_imag_hbm, fine.at[1]),
+            )
+        )
+    ]
+
+    barrier = pltpu.get_barrier_semaphore()
+    for axis in range(2):
+        at = lax.axis_index(axes[axis])
+        for hop in range(1, sizes[axis]):
+            peer = lax.rem(at + hop, sizes[axis])
+            pl.semaphore_signal(barrier, inc=1, device_id={axes[axis]: peer}, device_id_type=MESH)
+    for copy in factors + own_loads + [kept]:
+        copy.start()
+    pl.semaphore_wait(barrier, sizes[0] + sizes[1] - 2)
+    for copy in crossing + nearby + regroup:
+        copy.start()
+
+    for copy in factors:
+        copy.wait()
+
+    def table_rows(j, _):
+        rows = pl.ds(pl.multiple_of(j * ROOT, ROOT), ROOT)
+        coarse_r, coarse_i = coarse[0, pl.ds(j, 1), :], coarse[1, pl.ds(j, 1), :]
+        for at in range(0, columns, LANES):
+            real, imag = slice(at, at + LANES), slice(columns + at, columns + at + LANES)
+            cr, ci = coarse_r[:, real], coarse_i[:, real]
+            fr, fi = fine[0, :, real], fine[1, :, real]
+            table_high[rows, real], table_low[rows, real] = split(cr * fr - ci * fi)
+            table_high[rows, imag], table_low[rows, imag] = split(cr * fi + ci * fr)
+        return 0
+
+    lax.fori_loop(0, width // ROOT, table_rows, 0)
+    table_outs = [
+        pltpu.make_async_copy(table_high, high_hbm, table_sem.at[0]),
+        pltpu.make_async_copy(table_low, low_hbm, table_sem.at[1]),
+    ]
+    for copy in table_outs:
+        copy.start()
+
+    loadings = [
+        [basis_ref[slot_ref[c], q] for q in range(basis_ref.shape[1])] for c in range(slots)
+    ]
+    for c in range(slots):
+        for k in range(c + 1):
+            total = loadings[c][0] * loadings[k][0]
+            for q in range(1, basis_ref.shape[1]):
+                total = total + loadings[c][q] * loadings[k][q]
+            if c == k:
+                total = total + PRIOR_FLOOR
+            gram[c, k] = total
+            gram[k, c] = total
+
+    outs = []
+
+    def transform(pieces):
+        u = len(outs)
+        base = 0
+        for ref, first, rows in pieces:
+            here = slice(base, base + rows)
+            high_ref[here], low_ref[here] = split(ref[first : first + rows])
+            base += rows
+        if u >= 2:
+            outs[u - 2].wait()
+        dot = functools.partial(jnp.dot, preferred_element_type=jnp.float32)
+        for part in range(2):
+
+            def tile(t, _, part=part):
+                at = pl.ds(pl.multiple_of(t * TILE, TILE), TILE)
+                source = pl.ds(pl.multiple_of(part * columns + t * TILE, TILE), TILE)
+                weight = table_high[:, source]
+                high = high_ref[...]
+                result[u % 2, part, :, at] = (
+                    dot(high, weight) + dot(low_ref[...], weight) + dot(high, table_low[:, source])
+                )
+                return 0
+
+            lax.fori_loop(0, columns // TILE, tile, 0)
+        out = pltpu.make_async_copy(
+            result.at[u % 2], planes_hbm.at[:, pl.ds(u * unit, unit)], result_sem.at[u % 2]
+        )
+        out.start()
+        outs.append(out)
+
+    def pass_on(c):
+        crossing[c].wait_recv()
+        passing[c].start()
+
+    def far(c):
+        passing[c].wait_recv()
+        transform([(cross.at[c], 0, FINE), (passed.at[c], 0, FINE)])
+
+    for h in range(halves):
+        own_loads[h].wait()
+        transform([(mine, h * unit, unit)])
+    pass_on(0)
+    for h in range(halves):
+        nearby[h].wait_recv()
+        transform([(beside, h * unit, unit)])
+    for c in range(1, chunks - 1):
+        pass_on(c)
+        far(c - 1)
+    if chunks > 1:
+        far(chunks - 2)
+        pass_on(chunks - 1)
+
+    kept.wait()
+    for copy in regroup:
+        copy.wait_recv()
+    gram_values = [[gram[c, k] for k in range(slots)] for c in range(slots)]
+
+    def mix(step, _):
+        rows = pl.ds(pl.multiple_of(step // (width // LANES) * 8, 8), 8)
+        lanes = pl.ds(pl.multiple_of(step % (width // LANES) * LANES, LANES), LANES)
+        values = [cube[k, rows, lanes] for k in range(slots)]
+        for c in range(slots):
+            total = gram_values[c][0] * values[0]
+            for k in range(1, slots):
+                total = total + gram_values[c][k] * values[k]
+            cube[c, rows, lanes] = total
+        return 0
+
+    lax.fori_loop(0, block // 8 * (width // LANES), mix, 0, unroll=2)
+    prior_out = pltpu.make_async_copy(cube, prior_hbm, prior_sem.at[1])
+    prior_out.start()
+    far(chunks - 1)
+
+    for copy in crossing + nearby + passing + regroup:
+        copy.wait_send()
+    for copy in table_outs + outs[-2:] + [prior_out]:
+        copy.wait()
+
+
+def gather(basis, slot_channel, own, columns, length, sizes):
+    height, width = own.shape
+    factors = [jnp.asarray(factor) for factor in column_factors(width, length)]
+    unit = 2 * FINE
+    chunks = height // FINE
+    halves = height // unit
+    flights = 2 * chunks + halves
+    block = height // sizes[0]
+    anywhere = pl.BlockSpec(memory_space=pl.ANY)
+    scalars = pl.BlockSpec(memory_space=pltpu.SMEM)
+    table = jax.ShapeDtypeStruct((width, 2 * columns), jnp.bfloat16)
+    dma = pltpu.SemaphoreType.DMA
+    return pl.pallas_call(
+        functools.partial(gather_kernel, ("chan", "facet"), sizes),
+        in_specs=[scalars, scalars] + [anywhere] * 5,
+        out_specs=[anywhere] * 4,
+        out_shape=[
+            jax.ShapeDtypeStruct((2, sizes[1] * height, columns), jnp.float32),
+            jax.ShapeDtypeStruct((sizes[0], block, width), jnp.float32),
+            table,
+            table,
+        ],
+        scratch_shapes=[
+            pltpu.VMEM(table.shape, jnp.bfloat16),
+            pltpu.VMEM(table.shape, jnp.bfloat16),
+            pltpu.VMEM((2, width // ROOT, columns), jnp.float32),
+            pltpu.VMEM((2, ROOT, columns), jnp.float32),
+            pltpu.VMEM((height, width), jnp.float32),
+            pltpu.VMEM((height, width), jnp.float32),
+            pltpu.VMEM((chunks, FINE, width), jnp.float32),
+            pltpu.VMEM((chunks, FINE, width), jnp.float32),
+            pltpu.VMEM((unit, width), jnp.bfloat16),
+            pltpu.VMEM((unit, width), jnp.bfloat16),
+            pltpu.VMEM((2, 2, unit, columns), jnp.float32),
+            pltpu.VMEM((sizes[0], block, width), jnp.float32),
+            pltpu.SMEM((sizes[0], sizes[0]), jnp.float32),
+            dma((halves,)),
+            dma((4,)),
+            dma((2,)),
+            dma((2,)),
+            dma((2,)),
+            dma((flights,)),
+            dma((flights,)),
+            dma((sizes[0] - 1,)),
+            dma((sizes[0] - 1,)),
+        ],
+        compiler_params=pltpu.CompilerParams(
+            collective_id=2, has_side_effects=True, vmem_limit_bytes=60 << 20
+        ),
+        cost_estimate=SMALL,
+        name="gather",
+    )(basis, slot_channel, own, *factors)
+
+
 def scatter_kernel(axes, sizes, rows_hbm, high_hbm, low_hbm, prior_hbm, residual_hbm,
                    direction_hbm, applied_hbm, sums_ref, table_high, table_low, held, high_ref,
-                   low_ref, part, landed, beside, own, near, cross, stream, moment, mine, got,
-                   table_sem, held_sem, stream_sem, out_sem, send_sem, recv_sem, group_send,
-                   group_recv):
+                   low_ref, part, landed, beside, own, near, cross, prior, stream, moment,
+                   mine, got, table_sem, held_sem, stream_sem, out_sem, kept_sem, send_sem,
+                   recv_sem, group_send, group_recv, regroup_send, regroup_recv):
     width = table_high.shape[0]
     columns = held.shape[3]
     unit = held.shape[2]
@@ -584,10 +842,29 @@
         lax.fori_loop(0, FINE // 8, add, 0)
         crossing[c].start()
 
+    me = lax.axis_index(axes[0])
+    block = height // sizes[0]
+    mine_rows = pl.ds(pl.multiple_of(me * block, block), block)
+    kept = pltpu.make_async_copy(prior_hbm.at[me], prior.at[mine_rows], kept_sem)
+    kept.start()
+    regroup = []
+    for hop, peer in enumerate(peers(0)):
+        regroup.append(
+            pltpu.make_async_remote_copy(
+                src_ref=prior_hbm.at[peer],
+                dst_ref=prior.at[mine_rows],
+                send_sem=regroup_send.at[hop],
+                recv_sem=regroup_recv.at[hop],
+                device_id={axes[0]: peer},
+                device_id_type=MESH,
+            )
+        )
+    pl.semaphore_wait(barrier, sizes[0] + sizes[1] - 2)
+    for copy in regroup:
+        copy.start()
+
     for c in range(chunks):
         image(c, part.at[c])
-        if c == 0:
-            pl.semaphore_wait(barrier, sizes[0] + sizes[1] - 2)
         paired[c].start()
         if c:
             cross_over(c - 1)
@@ -599,7 +876,7 @@
     streams = [
         [
             pltpu.make_async_copy(source.at[chunk_rows(c)], stream.at[n], stream_sem.at[n])
-            for n, source in enumerate((prior_hbm, residual_hbm, direction_hbm))
+            for n, source in enumerate((residual_hbm, direction_hbm))
         ]
         for c in range(chunks)
     ]
@@ -609,8 +886,9 @@
         image(chunks + halves + h, own.at[pl.ds(h * unit, unit)])
 
     moment[...] = jnp.zeros_like(moment)
-    for copy in nearby:
+    for copy in nearby + regroup:
         copy.wait_recv()
+    kept.wait()
     outs = []
 
     def fold(total):
@@ -627,9 +905,9 @@
         def gather(i, _):
             at = pl.ds(pl.multiple_of(i * 8, 8), 8)
             here = pl.ds(pl.multiple_of(c * FINE + i * 8, 8), 8)
-            applied = own[here, :] + near[here, :] + cross[here, :] + stream[0, at, :]
+            applied = own[here, :] + near[here, :] + cross[here, :] + prior[here, :]
             own[here, :] = applied
-            residual, direction = stream[1, at, :], stream[2, at, :]
+            residual, direction = stream[0, at, :], stream[1, at, :]
             moment[0] += fold(residual * residual)
             moment[1] += fold(direction * applied)
             moment[2] += fold(residual * applied)
@@ -647,7 +925,7 @@
         outs.append(out)
 
     group_sum(axes, sizes, moment[...], sums_ref, mine, got, group_send, group_recv)
-    for copy in paired + crossing + nearby:
+    for copy in paired + crossing + nearby + regroup:
         copy.wait_send()
     for out in outs:
         out.wait()
@@ -684,18 +962,22 @@
             whole,
             whole,
             whole,
-            pltpu.VMEM((3, FINE, width), jnp.float32),
+            whole,
+            pltpu.VMEM((2, FINE, width), jnp.float32),
             pltpu.VMEM(shape, jnp.float32),
             pltpu.VMEM((2,) + shape, jnp.float32),
             pltpu.VMEM((hops,) + shape, jnp.float32),
             dma((2, width // TILE)),
             dma((2,)),
-            dma((3,)),
+            dma((2,)),
             dma((chunks,)),
+            dma,
             dma((flights,)),
             dma((flights,)),
             dma((hops,)),
             dma((hops,)),
+            dma((sizes[0] - 1,)),
+            dma((sizes[0] - 1,)),
         ],
         compiler_params=pltpu.CompilerParams(
             collective_id=1, has_side_effects=True, vmem_limit_bytes=60 << 20
@@ -754,28 +1036,6 @@
     per_facet = height // FINE
     barrier = lax.optimization_barrier
 
-    chunks = [own[at * FINE : (at + 1) * FINE] for at in range(per_facet)]
-    crossed = [swap_pairs(chunk, facets, top) for chunk in chunks]
-
-    def spread(block, key):
-        blocks = {key: block}
-        bit = top // 2
-        while bit:
-            blocks.update({k ^ bit: swap_pairs(blocks[k], facets, bit) for k in list(blocks)})
-            bit //= 2
-        return blocks
-
-    near = spread(own, 0)
-
-    cube = own.reshape(channel_count, height // channel_count, width)
-    regrouped = lax.all_to_all(cube, "chan", split_axis=0, concat_axis=0, tiled=True)
-    one_hot = (
-        slot_channel[:, None] == jnp.arange(channel_count, dtype=jnp.int32)[None, :]
-    ).astype(jnp.float32)
-    loadings = jnp.dot(one_hot, basis, precision=HIGHEST)
-    gram = jnp.einsum("cq,dq->cd", loadings, loadings, precision=HIGHEST)
-    gram = gram + PRIOR_FLOOR * jnp.eye(channel_count, dtype=jnp.float32)
-
     groups = []
     if per_facet > 1:
         groups += [[(key, s) for s in range(per_facet)] for key in range(top)]
@@ -787,6 +1047,36 @@
     for at, (key, s) in enumerate(entry for entries in groups for entry in entries):
         slot_of[key, s] = at
     slots = jnp.asarray(slot_of)[jnp.arange(facets, dtype=jnp.int32) ^ place].reshape(-1)
+
+    sizes = (lax.axis_size("chan"), facets)
+    if facets == 4 and per_facet % 2 == 0 and height % (8 * sizes[0]) == 0:
+        planes, local, *tables = gather(basis, slot_channel, own, columns, length, sizes)
+        rows = row_pass(planes, spectra[0], slots)
+        applied, sums = scatter(rows, tables, local, residual[0], own, sizes)
+        results = update(sums, solution[0], residual[0], own, applied)
+        return tuple(result[None] for result in results)
+
+    chunks = [own[at * FINE : (at + 1) * FINE] for at in range(per_facet)]
+    crossed = [swap_pairs(chunk, facets, top) for chunk in chunks]
+
+    def spread(block, key):
+        blocks = {key: block}
+        bit = top // 2
+        while bit:
+            blocks.update({k ^ bit: swap_pairs(blocks[k], facets, bit) for k in list(blocks)})
+            bit //= 2
+        return blocks
+
+    near = spread(own, 0)
+
+    cube = own.reshape(channel_count, height // channel_count, width)
+    regrouped = lax.all_to_all(cube, "chan", split_axis=0, concat_axis=0, tiled=True)
+    one_hot = (
+        slot_channel[:, None] == jnp.arange(channel_count, dtype=jnp.int32)[None, :]
+    ).astype(jnp.float32)
+    loadings = jnp.dot(one_hot, basis, precision=HIGHEST)
+    gram = jnp.einsum("cq,dq->cd", loadings, loadings, precision=HIGHEST)
+    gram = gram + PRIOR_FLOOR * jnp.eye(channel_count, dtype=jnp.float32)
 
     tables = width_table(width, columns, length, place)
     planes = None
@@ -811,12 +1101,6 @@
             prior = prior.reshape(height, width)
 
     rows = row_pass(planes, spectra[0], slots)
-
-    sizes = (lax.axis_size("chan"), facets)
-    if facets == 4 and per_facet % 2 == 0:
-        applied, sums = scatter(rows, tables, prior, residual[0], own, sizes)
-        results = update(sums, solution[0], residual[0], own, applied)
-        return tuple(result[None] for result in results)
 
     arrived = {}
     near_sums = {}

time: 367 us -> 329 us (0.90)
  starting transfers between devices: 18.1 us -> 0 us
  waiting for transfers between devices: 6.9 us -> 0 us
  local copies, waits for them, and re-layouts: 7.31 us -> 1.85 us
  Pallas kernels: 331 us -> 326 us
    all_to_all x2 -> x0, starting transfers between devices: 13.4 us -> none  [the longest x1 7.29 us: body(): lax.all_to_all(cube, 'chan', split_axis=0, concat_axis=0, tiled=True)]
    ppermute x9 -> x0, waiting for transfers between devices: 6.9 us -> none  [swap_pairs(): return lax.ppermute(array, 'facet', pairs)]
    ppermute x9 -> x0, starting transfers between devices: 4.66 us -> none  [swap_pairs(): return lax.ppermute(array, 'facet', pairs)]
    slice x1 -> x0, local copies, waits for them, and re-layouts: 3.94 us -> none  [body(): chunks = [own[at * FINE:(at + 1) * FINE] for at in range(per_facet)]]
    pallas_call x8 -> x1, Pallas kernels: 113 us -> 113 us  [gather(): pl.pallas_call(functools.partial(gather_kernel, ('chan', 'facet'), sizes)...]
  transfers between devices with their start and end apart: 11 -> 0, of which waited for: 2 -> 0; matrix products, arithmetic and copies ran while one was open for 2% -> 0% of each run, Pallas kernels for 51% -> 0%
where the time goes in v3:
time: 329 us
  Pallas kernels  326 us (99%)
    pallas_call x1, Pallas kernels, scatter(): pl.pallas_call(functools.partial(scatter_kernel, ('chan', 'facet'), sizes...  123 us
    pallas_call x1, Pallas kernels, gather(): pl.pallas_call(functools.partial(gather_kernel, ('chan', 'facet'), sizes)...  113 us
    pallas_call x1, Pallas kernels, row_pass(): pl.pallas_call(row_kernel, grid_spec=pltpu.PrefetchScalarGridSpec(num_sca...  78.5 us
    pallas_call x1, Pallas kernels, update(): pl.pallas_call(update_kernel, grid=(height // step,), in_specs=[pl.BlockS...  12.2 us

profile of v3, /device:TPU:0, one launch (start us, length us, event | category | flops | bytes accessed | tf_op | source)
XLA Modules:
  0.0 328.8 jit_solution(7140563096604027970)
XLA Ops:
  0.7 1.2 gather_fusion
  1.9 0.6 reshape.25.slot_ref
  2.5 113.0 %gather.7 = (f32[2,2048,1024]{2,1,0:T(8,128)}, f32[8,64,2048]{2,1,0:T(8,128)}, bf16[2048,2048]{1,0:T(8,128)(2,1)}, bf16[2048,2048]{1,0:T(8,128)(2,1)}) custom-call(f32[8,8]{1,0:T(8,128)} %basis_ref.1, s32[8]{0:T(128)} %slot_ref.1, f32[512,2048]{1,0:T(8,128)} %bitcast.11, f32[32,4096]{1,0:T(8,128)} %constant.27.clone.coarse_real_hbm, ...), custom_call_target="tpu_custom_call" | custom-call | flops 1 | bytes 1 | tf_op jit(solution)/shard_map/gather/pallas_call | solution.py:693
  115.5 78.5 %row_pass.1.rows_hbm = f32[2,2048,1024]{2,1,0:T(8,128)} custom-call(s32[16]{0:T(128)} %reshape.25.slot_ref, f32[2,2048,1024]{2,1,0:T(8,128)} %get-tuple-element.12.planes_ref, f32[4096,1024]{1,0:T(8,128)} %bitcast.9, f32[4096,1024]{1,0:T(8,128)} %bitcast.10, bf16[32,256,256]{2,1,0:T(8,128)(2,1)} %constant.31.clone.refs_2_, ...), custom_call_target="tpu_custom_call" | custom-call | flops 1 | bytes 1 | tf_op jit(solution)/shard_map/row_pass/pallas_call | solution.py:184
  193.9 122.6 %scatter.1 = (f32[512,2048]{1,0:T(8,128)}, f32[4,8,128]{2,1,0:T(8,128)}) custom-call(f32[2,2048,1024]{2,1,0:T(8,128)} %row_pass.1.rows_hbm, bf16[2048,2048]{1,0:T(8,128)(2,1)} %get-tuple-element.13.high_hbm, bf16[2048,2048]{1,0:T(8,128)(2,1)} %get-tuple-element.14.low_hbm, f32[8,64,2048]{2,1,0:T(8,128)} %get-tuple-element.15.prior_hbm, ...), custom_call_target="tpu_custom_call" | custom-call | flops 1 | bytes 1 | tf_op jit(solution)/shard_map/scatter/pallas_call | solution.py:945
  316.6 12.2 %update.1 = (f32[512,2048]{1,0:T(8,128)}, f32[512,2048]{1,0:T(8,128)}, f32[512,2048]{1,0:T(8,128)}) custom-call(f32[4,8,128]{2,1,0:T(8,128)} %get-tuple-element.16.sum_ref, f32[512,2048]{1,0:T(8,128)} %bitcast.16, f32[512,2048]{1,0:T(8,128)} %bitcast.15, f32[512,2048]{1,0:T(8,128)} %bitcast.13, f32[512,2048]{1,0:T(8,128)} %get-tuple-element.17.applied_ref), custom_call_target="tpu_custom_call" | custom-call | flops 1 | bytes 1 | tf_op jit(solution)/shard_map/update/pallas_call | solution.py:1011
  (2 shorter events, 0.0 us)
